TPU v7x, 32 devices: a whole 2x2x4 slice. The times are simulated.
32 devices in a mesh: dp: 8 (over y, x, core), mp: 4 (over z).
Axes of the slice: x: 2, y: 2, z: 4, core: 2. Of those that a mesh axis runs over, the one named last changes fastest.
Arguments:
- features: bfloat16 [9216, 7168], P(('dp', 'mp')), may hold values from -6 to 6
- online_head: bfloat16 [7168, 128], P('dp'), may hold values from -0.0625 to 0.0625
- target_head: bfloat16 [7168, 128], P('dp'), may hold values from -0.0625 to 0.0625
- action_bin: int32 [9216], P(('dp', 'mp')), may hold values from 0 to 127
- next_index: int32 [9216], P(('dp', 'mp')), may hold values from 0 to 9215, as said below
- reward: float32 [9216], P(('dp', 'mp')), may hold values from 0 to 1
- terminal: int32 [9216], P(('dp', 'mp')), may hold values 0 or 1
Outputs:
- td_error: float32 [9216], P(('dp', 'mp'))
- head_grad: float32 [7168, 128], P('dp')
Inputs may be any that keep to these rules, and one draw needn't show every extreme that they name: Where t mod 8 < 7, next_index[t] = t + 1; otherwise next_index[t] is a multiple of 8 inside the same aligned block of 1152 tokens as t.
All inputs are finite; a program needn't handle non-finite values. No bound on the sum of `terminal` on one device may be relied on, other than what follows from the above.
Results may differ from a plain program's by a relative error of at most 0.0029.
Values may be sent and summed in bfloat16 or wider, within the bound.
No kernel may reach another device: no remote copies, remote signals or barrier semaphores. Data moves between devices by JAX's collectives and lax.ppermute only.
A program may use at most 64 MiB of HBM per device.

v0:
```python
import math

import jax
import jax.numpy as jnp
from jax import lax
from jax.sharding import PartitionSpec as P

ADIM = 8


DISCOUNT = 0.98
CONSERVATIVE = 2.0


def body(features, online_head, target_head, action_bin, next_index, reward, terminal):
    tok_rows = features.shape[0]
    bin_count = online_head.shape[1]
    group_size = tok_rows * lax.axis_size("mp")
    all_tokens = group_size * lax.axis_size("dp")
    online_full = lax.all_gather(online_head, "dp", axis=0, tiled=True)
    columns = features
    target_logits = jnp.dot(
        columns,
        lax.all_gather(target_head, "dp", axis=0, tiled=True),
        preferred_element_type=jnp.float32,
    )
    best_value = jnp.max(target_logits, axis=1)
    local_next = next_index - lax.axis_index("dp") * group_size
    step_dim = jnp.arange(tok_rows, dtype=jnp.int32) % ADIM
    is_last = step_dim == ADIM - 1
    group_best = lax.all_gather(best_value, "mp", axis=0, tiled=True)
    next_best = jnp.take(group_best, local_next, axis=0)
    bootstrap = reward + DISCOUNT * (1.0 - terminal.astype(jnp.float32)) * next_best
    target_value = jnp.where(is_last, bootstrap, next_best)
    q_values = jnp.dot(features, online_full, preferred_element_type=jnp.float32)
    onehot = (jnp.arange(bin_count, dtype=jnp.int32)[None, :] == action_bin[:, None]).astype(
        jnp.float32
    )
    td_error = jnp.sum(q_values * onehot, axis=1) - target_value
    grad_scale = 1.0 / math.sqrt(all_tokens)
    q_grad = (
        grad_scale
        * (
            onehot * td_error[:, None]
            + (1.0 - onehot) * (CONSERVATIVE / (bin_count - 1)) * q_values
        )
    ).astype(jnp.bfloat16)
    columns = features
    grad_owned = lax.psum_scatter(
        lax.dot_general(
            columns, q_grad, (((0,), (0,)), ((), ())), preferred_element_type=jnp.float32
        ),
        "dp",
        scatter_dimension=0,
        tiled=True,
    )
    head_grad = lax.psum(grad_owned, "mp")
    return (td_error, head_grad)


def solution(mesh):
    placed = (
        P(("dp", "mp"), None),
        P("dp", None),
        P("dp", None),
        P(("dp", "mp")),
        P(("dp", "mp")),
        P(("dp", "mp")),
        P(("dp", "mp")),
    )
    return jax.shard_map(
        body,
        mesh=mesh,
        in_specs=placed,
        out_specs=(P(("dp", "mp")), P("dp", None)),
        check_vma=False,
    )
```

profile of v0, /device:TPU:0, one launch (start us, length us, event | category | flops | bytes accessed | tf_op | source)
XLA Modules:
  0.0 172.3 jit_solution(15020526922892306121)
XLA Ops:
  7.2 0.0 all-gather.5.cloned.1.call-start
  7.2 0.7 all-gather.5.cloned.1.call-update
  7.9 0.0 all-gather.3.cloned.1.call-start
  7.9 0.7 all-gather.3.cloned.1.call-update
  8.6 0.0 reduce-scatter.2.cloned.1.call-start
  8.7 1.2 dynamic-slice
  10.6 0.7 compare_select_fusion
  11.3 0.0 copy-start.2
  11.3 28.0 %all-gather.5.cloned.1.call-done = bf16[7168,128]{1,0:T(8,128)(2,1)} async-done(((bf16[896,128]{1,0:T(8,128)(2,1)}), bf16[7168,128]{1,0:T(8,128)(2,1)}) %all-gather.5.cloned.1.call-update) | async-done | bytes 1835024 | tf_op jit(solution)/shard_map/all_gather | solution.py:24
  39.3 4.1 %convolution_reduce_fusion = f32[288]{0:T(512)S(1)} fusion(bf16[288,7168]{1,0:T(8,128)(2,1)} %param.7, bf16[7168,128]{1,0:T(8,128)(2,1)} %all-gather.5.cloned.1.call-done), kind=kOutput, calls=%fused_computation.2 | convolution fusion | flops 528518880 | bytes 5964928 | tf_op jit(solution)/shard_map/dot_general | solution.py:22
  43.4 0.3 dynamic-update-slice
  43.7 11.8 %all-reduce = f32[1152]{0:T(1024)S(1)} all-reduce(f32[1152]{0:T(1024)S(1)} %dynamic-update-slice), channel_id=1, replica_groups=mesh['dp'=8,'mp'=4] {'mp'}, use_global_device_ids=true, to_apply=%add | all-reduce | flops 1152 | bytes 9216
  55.5 2.2 %gather_fusion = f32[288]{0:T(512)S(1)} fusion(f32[1152]{0:T(1024)S(1)} %all-reduce, s32[1024]{0:T(1024)S(1)} %pad_clamp_fusion), kind=kCustom, calls=%fused_computation | custom fusion | bytes 3456 | tf_op jit(solution)/shard_map/jit(_take)/gather | solution.py:32
  57.7 0.0 copy-start.3
  57.7 0.0 copy-start.4
  57.8 0.0 copy-start.5
  57.8 10.1 %all-gather.3.cloned.1.call-done = bf16[7168,128]{1,0:T(8,128)(2,1)} async-done(((bf16[896,128]{1,0:T(8,128)(2,1)}), bf16[7168,128]{1,0:T(8,128)(2,1)}) %all-gather.3.cloned.1.call-update) | async-done | bytes 1835024 | tf_op jit(solution)/shard_map/all_gather | solution.py:20
  67.9 0.0 copy-done.2
  67.9 0.0 copy-start
  67.9 4.2 %select_reduce_fusion = (f32[288]{0:T(512)S(1)}, f32[288,128]{1,0:T(8,128)S(1)}) fusion(s32[288]{0:T(512)S(1)} %copy-done.2, bf16[288,7168]{1,0:T(8,128)(2,1)} %param.7, bf16[7168,128]{1,0:T(8,128)(2,1)} %all-gather.3.cloned.1.call-done), kind=kOutput, calls=%fused_computation.4 | convolution fusion | flops 528592608 | bytes 6113536 | tf_op jit(solution)/shard_map/dot_general | solution.py:35
  72.1 0.0 copy-done.3
  72.1 0.0 copy-done.4
  72.1 0.0 copy-done.5
  72.2 0.0 copy-start.1
  72.2 0.0 copy-done
  72.2 3.1 %convolution_bitcast_fusion = f32[7168,128]{0,1:T(8,128)} fusion(bf16[288,7168]{1,0:T(8,128)(2,1)S(1)} %copy-done, f32[288,128]{1,0:T(8,128)S(1)} %get-tuple-element.7, f32[288]{0:T(512)S(1)} %select_subtract_fusion, s32[288]{0:T(512)S(1)} %copy-done.2), kind=kOutput, calls=%fused_computation.1 | convolution fusion | flops 528814080 | bytes 7948544 | tf_op jit(solution)/shard_map/dot_general | solution.py:50
  75.3 0.0 copy-done.1
  75.3 0.0 reduce-scatter.2.cloned.1.call-update
  75.3 0.0 all-reduce.3.cloned.1.call-start
  75.3 48.7 %reduce-scatter.2.cloned.1.call-done = f32[896,128]{0,1:T(8,128)} async-done(((f32[7168,128]{0,1:T(8,128)}), f32[896,128]{0,1:T(8,128)}) %reduce-scatter.2.cloned.1.call-update) | async-done | bytes 458768 | tf_op jit(solution)/shard_map/reduce_scatter | solution.py:49
  124.0 0.0 all-reduce.3.cloned.1.call-update
  124.0 39.8 %all-reduce.3.cloned.1.call-done = f32[896,128]{0,1:T(8,128)} async-done(((f32[896,128]{0,1:T(8,128)}), f32[896,128]{0,1:T(8,128)}) %all-reduce.3.cloned.1.call-update) | async-done | bytes 458768 | tf_op jit(solution)/shard_map/psum | solution.py:57
  163.8 2.0 %copy.10 = f32[896,128]{1,0:T(8,128)} copy(f32[896,128]{0,1:T(8,128)} %all-reduce.3.cloned.1.call-done) | data formatting | bytes 917504
  (3 shorter events, 0.0 us)
Async XLA Ops:
  7.2 32.1 %all-gather.5.cloned.1.call-start = ((), (), s32[]{:S(2)}) async-start(), calls=%async_computation.2 | async-start | bytes 2064384 | tf_op jit(solution)/shard_map/all_gather | solution.py:24
  7.9 60.0 %all-gather.3.cloned.1.call-start = ((), (), s32[]{:S(2)}) async-start(), calls=%async_computation.1 | async-start | bytes 2064384 | tf_op jit(solution)/shard_map/all_gather | solution.py:20
  8.6 115.3 %reduce-scatter.2.cloned.1.call-start = ((), (), s32[]{:S(2)}) async-start(), calls=%async_computation.3 | async-start | bytes 4128768 | tf_op jit(solution)/shard_map/reduce_scatter | solution.py:49
  11.3 56.6 %copy-start.2 = (s32[288]{0:T(512)S(1)}, s32[288]{0:T(512)}, u32[]{:S(2)}) copy-start(s32[288]{0:T(512)} %param.10) | copy-start | bytes 3460
  57.7 14.4 %copy-start.3 = (s32[288]{0:T(512)S(1)}, s32[288]{0:T(512)}, u32[]{:S(2)}) copy-start(s32[288]{0:T(512)} %param.11) | copy-start | bytes 3460
  57.7 14.4 %copy-start.4 = (f32[288]{0:T(512)S(1)}, f32[288]{0:T(512)}, u32[]{:S(2)}) copy-start(f32[288]{0:T(512)} %param.12) | copy-start | bytes 3460
  57.8 14.4 %copy-start.5 = (s32[288]{0:T(512)S(1)}, s32[288]{0:T(512)}, u32[]{:S(2)}) copy-start(s32[288]{0:T(512)} %param.13) | copy-start | bytes 3460
  67.9 4.3 %copy-start = (bf16[288,7168]{1,0:T(8,128)(2,1)S(1)}, bf16[288,7168]{1,0:T(8,128)(2,1)}, u32[]{:S(2)}) copy-start(bf16[288,7168]{1,0:T(8,128)(2,1)} %param.7) | copy-start | bytes 12386308
  72.2 3.1 %copy-start.1 = (f32[288]{0:T(512)}, f32[288]{0:T(512)S(1)}, u32[]{:S(2)}) copy-start(f32[288]{0:T(512)S(1)} %select_subtract_fusion) | copy-start | bytes 3460
  75.3 88.5 %all-reduce.3.cloned.1.call-start = ((), (), s32[]{:S(2)}) async-start(), calls=%async_computation.4 | async-start | bytes 917504 | tf_op jit(solution)/shard_map/psum | solution.py:57
Sparse Core Ops, SparseCore 0:
  9.9 29.3 all-gather.4
  41.2 26.6 all-gather.2
  75.4 48.5 reduce-scatter.1
  126.2 37.5 all-reduce.2
where the time goes:
time: 173 us; the launch traced here: 172 us
  waiting for transfers between devices  128 us (74%)
  between operations  14.5 us (8%)
  blocking collectives  11.8 us (7%)
  matrix products  11.4 us (7%)
  local copies, waits for them, and re-layouts  5.78 us (3%)
    reduce_scatter x1, waiting for transfers between devices, body(): lax.psum_scatter(lax.dot_general(columns, q_grad, (((0,), (0,)), ((), ())...  48.7 us
    psum x1, waiting for transfers between devices, body(): head_grad = lax.psum(grad_owned, 'mp')  39.8 us
    all_gather x1, waiting for transfers between devices, body(): lax.all_gather(target_head, 'dp', axis=0, tiled=True)  28 us
    unnamed x1, blocking collectives  11.8 us
    all_gather x1, waiting for transfers between devices, body(): online_full = lax.all_gather(online_head, 'dp', axis=0, tiled=True)  10.1 us
    dot_general x1, matrix products, body(): jnp.dot(features, online_full, preferred_element_type=jnp.float32)  4.22 us
    dot_general x1, matrix products, body(): jnp.dot(columns, lax.all_gather(target_head, 'dp', axis=0, tiled=True), p...  4.08 us
    unnamed x16, local copies, waits for them, and re-layouts  3.54 us
  transfers between devices with their start and end apart: 4, of which 4 were waited for; matrix products, arithmetic and copies ran while one was open for 5% of the time, Pallas kernels for 0%

commit v1 on v0

--- a/solution.py
+++ b/solution.py
@@ -1,18 +1,207 @@
+import functools
 import math
 
 import jax
 import jax.numpy as jnp
 from jax import lax
+from jax.experimental import pallas as pl
+from jax.experimental.pallas import tpu as pltpu
 from jax.sharding import PartitionSpec as P
 
+
 ADIM = 8
+LANES = 128
 
 
 DISCOUNT = 0.98
 CONSERVATIVE = 2.0
 
 
-def body(features, online_head, target_head, action_bin, next_index, reward, terminal):
+f32, bf16 = jnp.float32, jnp.bfloat16
+VMEM = pl.BlockSpec(memory_space=pltpu.VMEM)
+ANY = pl.BlockSpec(memory_space=pl.ANY)
+MIB = 1 << 20
+SMEM = pl.BlockSpec(memory_space=pltpu.SMEM)
+
+
+def across(value, mask):
+    count = lax.axis_size("dp")
+    return lax.ppermute(value, "dp", [(i, i ^ mask) for i in range(count)])
+
+
+def shifted(value, step):
+    count = lax.axis_size("mp")
+    return lax.ppermute(value, "mp", [(i, (i + step) % count) for i in range(count)])
+
+
+def call(kernel, outs, *args, smem=0, scratch=()):
+    return pl.pallas_call(
+        kernel,
+        out_shape=outs,
+        scratch_shapes=scratch,
+        in_specs=[SMEM] * smem + [VMEM] * (len(args) - smem),
+        out_specs=jax.tree.map(lambda _: VMEM, outs),
+        compiler_params=pltpu.CompilerParams(vmem_limit_bytes=16 * MIB),
+    )(*args[:smem], *(kept(a) for a in args[smem:]))
+
+
+def kept(value):
+    return pltpu.with_memory_space_constraint(value, pltpu.VMEM)
+
+
+def shape(*dims, dtype=f32):
+    return pltpu.VMEM(dims, dtype)
+
+
+def relay_order(chips):
+    return sorted(range(1, chips), key=lambda o: (bin(o).count("1"), o))
+
+
+def direct_hops(shard, chips):
+    return {0: (shard,), **{o: (across(shard, 2 * o),) for o in relay_order(chips)}}
+
+
+def first_hops(shard, chips):
+    return {o: (across(shard, 2 * o),) for o in relay_order(chips) if o & (o - 1) == 0}
+
+
+def halves_kernel(*refs):
+    count = len(refs) // 3
+    for ref, first_ref, second_ref in zip(refs[:count], refs[count::2], refs[count + 1 :: 2]):
+        half = first_ref.shape[0]
+        first_ref[...] = ref[:half]
+        second_ref[...] = ref[half:]
+
+
+def relayed(shard, held, chips):
+    half = shape(shard.shape[0] // 2, shard.shape[1], dtype=shard.dtype)
+    hops = [h[0] for h in held.values()]
+    parts = call(halves_kernel, (half,) * (2 * len(hops)), *hops)
+    split = dict(zip(held, zip(parts[::2], parts[1::2])))
+    held = {0: (shard,), **held}
+    for offset in relay_order(chips):
+        if offset in held:
+            continue
+        low = offset & -offset
+        high = 1 << (offset.bit_length() - 1)
+        first = split.get(offset ^ high, held[offset ^ high])[0]
+        second = split.get(offset ^ low, held[offset ^ low])[1]
+        held[offset] = (across(first, 2 * high), across(second, 2 * low))
+    return held
+
+
+def column(ref, at_ref, offset, width):
+    return ref.at[:, pl.ds(pl.multiple_of(at_ref[offset] * width, width), width)]
+
+
+def cut_kernel(at_ref, features_ref, sent_ref):
+    chips, _, width = sent_ref.shape
+    for j in range(chips):
+        sent_ref[j] = column(features_ref, at_ref, chips + j, width)[...]
+
+
+def turn_kernel(at_ref, features_ref, theirs_ref, out_ref):
+    for j in range(theirs_ref.shape[0]):
+        mine = column(features_ref, at_ref, j, theirs_ref.shape[2])[...]
+        both = jnp.concatenate([mine, theirs_ref[j]], axis=0)
+        out_ref[j] = both.T
+
+
+def logits_kernel(offsets, has_start, at_ref, features_ref, theirs_ref, *refs):
+    pieces, out_ref = refs[: len(offsets)], refs[-1]
+    width = theirs_ref.shape[2]
+    for side in range(2):
+        total = refs[-2][side] if has_start else None
+        for (offset, at), piece in zip(offsets, pieces):
+            cols = (theirs_ref.at[offset], column(features_ref, at_ref, offset, width))[1 - side]
+            part = jnp.dot(
+                cols[:, at : at + piece.shape[0]], piece[...], preferred_element_type=f32
+            )
+            total = part if total is None else total + part
+        out_ref[side] = total
+
+
+def partial_logits(at, features, theirs, held, start=None):
+    offsets, pieces = [], []
+    for offset, parts in held.items():
+        row = 0
+        for part in parts:
+            offsets.append((offset, row))
+            pieces.append(part)
+            row += part.shape[0]
+    out = shape(2, features.shape[0], pieces[0].shape[1])
+    extra = () if start is None else (start,)
+    kernel = functools.partial(logits_kernel, tuple(offsets), start is not None)
+    return call(kernel, out, at, features, theirs, *pieces, *extra, smem=1)
+
+
+def best_kernel(part_ref, other_ref, best_ref, firsts_ref):
+    tokens = part_ref.shape[1]
+    lanes = firsts_ref.shape[1]
+    token = lax.broadcasted_iota(jnp.int32, (tokens, lanes), 0)
+    lane = lax.broadcasted_iota(jnp.int32, (tokens, lanes), 1)
+    for side in range(2):
+        best = jnp.max(part_ref[side] + other_ref[1 - side], axis=1, keepdims=True)
+        best_ref[side] = jnp.broadcast_to(best, best_ref.shape[1:])
+        picked = jnp.where(token == ADIM * lane, best, 0.0)
+        firsts_ref[side : side + 1] = jnp.sum(picked, axis=0, keepdims=True)
+
+
+def goal_kernel(sources_at, at_ref, best_ref, scalar_ref, other_ref, *refs):
+    *firsts, out_ref, rows_ref = refs
+    tokens = best_ref.shape[1]
+    lanes = firsts[0].shape[1]
+    steps = tokens // ADIM
+    rows_ref[...] = jnp.zeros_like(rows_ref)
+    rows_ref[:4, :tokens] = scalar_ref[...]
+    rows_ref[4:, :tokens] = other_ref[...]
+    columns = rows_ref[...].T
+    lane = lax.broadcasted_iota(jnp.int32, (tokens, lanes), 1)
+    token = lax.broadcasted_iota(jnp.int32, (tokens, 1), 0)
+    is_last = (token & (ADIM - 1)) == ADIM - 1
+    for side in range(2):
+        action, nxt, rew, term = (
+            columns[:tokens, 4 * side + i : 4 * side + i + 1] for i in range(4)
+        )
+        step_at = nxt.astype(jnp.int32) >> (ADIM.bit_length() - 1)
+        jumped = jnp.zeros((tokens, lanes), f32)
+        for k, table in enumerate(firsts):
+            label = lane + at_ref[sources_at + k] * steps
+            hit = (label == step_at) & (lane < steps)
+            jumped = jnp.where(hit, table[side : side + 1], jumped)
+        jumped = jnp.sum(jumped, axis=1, keepdims=True)
+        following = pltpu.roll(best_ref[side], tokens - 1, 0)[:, :1]
+        bootstrap = rew + DISCOUNT * (1.0 - term) * jumped
+        goal = jnp.where(is_last, bootstrap, following)
+        first = lax.broadcasted_iota(jnp.int32, (tokens, LANES), 1) == 0
+        out_ref[side] = jnp.where(first, goal, action)
+
+
+def grad_kernel(grad_scale, at, part_ref, other_ref, goal_ref, cols_ref, grad_ref, error_ref, out_ref):
+    tokens, bins = part_ref.shape[1:]
+    lane = lax.broadcasted_iota(jnp.int32, (tokens, bins), 1)
+    for side in range(2):
+        values = part_ref[side] + other_ref[1 - side]
+        goal = goal_ref[side]
+        taken = lane == goal[:, 1:2].astype(jnp.int32)
+        td_error = jnp.sum(jnp.where(taken, values, 0.0), axis=1, keepdims=True) - goal[:, :1]
+        grad = grad_scale * jnp.where(taken, td_error, (CONSERVATIVE / (bins - 1)) * values)
+        grad_ref[side * tokens : (side + 1) * tokens] = grad.astype(bf16)
+        if side == 0:
+            error_ref[...] = jnp.broadcast_to(td_error, error_ref.shape)
+    out_ref[...] = jnp.dot(cols_ref[at], grad_ref[...], preferred_element_type=f32).astype(
+        out_ref.dtype
+    )
+
+
+def term_kernel(offsets, cols_ref, grad_ref, *outs):
+    for offset, out_ref in zip(offsets, outs):
+        out_ref[...] = jnp.dot(
+            cols_ref[offset], grad_ref[...], preferred_element_type=f32
+        ).astype(out_ref.dtype)
+
+
+def plain_body(features, online_head, target_head, action_bin, next_index, reward, terminal):
     tok_rows = features.shape[0]
     bin_count = online_head.shape[1]
     group_size = tok_rows * lax.axis_size("mp")
@@ -58,6 +247,107 @@
     return (td_error, head_grad)
 
 
+def body(features, online_head, target_head, action_bin, next_index, reward, terminal):
+    tokens = features.shape[0]
+    head_rows, bins = online_head.shape
+    mp_size = lax.axis_size("mp")
+    dp_size = lax.axis_size("dp")
+    if head_rows % LANES or head_rows % (16 * mp_size) or dp_size & (dp_size - 1):
+        return plain_body(
+            features, online_head, target_head, action_bin, next_index, reward, terminal
+        )
+    chips = dp_size // 2
+    group_size = tokens * mp_size
+    all_tokens = group_size * dp_size
+    dp_at = lax.axis_index("dp")
+    mp_at = lax.axis_index("mp")
+    core, chip = dp_at & 1, dp_at >> 1
+
+    target_held = direct_hops(target_head, chips)
+    online_hops = first_hops(online_head, chips)
+
+    offset = jnp.arange(chips, dtype=jnp.int32)
+    owner = 2 * (chip ^ offset)
+    at, other_at = owner + core, owner + 1 - core
+    sources = mp_at - jnp.arange(mp_size, dtype=jnp.int32)
+    sources = jnp.where(sources < 0, sources + mp_size, sources)
+    at = jnp.concatenate([at, other_at, sources])
+    block = shape(chips, tokens, head_rows, dtype=features.dtype)
+    sent = call(cut_kernel, block, at, features, smem=1)
+    theirs = across(sent, 1)
+    scalars = jnp.stack(
+        [
+            action_bin.astype(f32),
+            (next_index - dp_at * group_size).astype(f32),
+            reward,
+            terminal.astype(f32),
+        ]
+    )
+    scalars = (scalars, across(scalars, 1))
+    out = shape(chips, head_rows, 2 * tokens, dtype=features.dtype)
+    cols_turned = call(turn_kernel, out, at, features, theirs, smem=1)
+    online_held = relayed(online_head, online_hops, chips)
+
+    last = chips - 1
+    both = shape(2, tokens, bins)
+
+    def logits(held):
+        early = {o: p for o, p in held.items() if o != last}
+        part = partial_logits(at, features, theirs, early)
+        part = partial_logits(at, features, theirs, {last: held[last]}, part)
+        return part, across(part, 1)
+
+    parts = logits(target_held)
+    lanes = -(-(tokens // ADIM) // LANES) * LANES
+    best, firsts = call(best_kernel, (both, shape(2, lanes)), *parts)
+    tables = [firsts]
+    for k in range(1, mp_size):
+        tables.append(shifted(firsts, k))
+    goal = call(
+        functools.partial(goal_kernel, 2 * chips), both, at, best, *scalars, *tables, smem=1,
+        scratch=[pltpu.VMEM((8, -(-tokens // LANES) * LANES), f32)],
+    )
+
+    parts = logits(online_held)
+    grad_scale = 1.0 / math.sqrt(all_tokens)
+    block = shape(head_rows, bins, dtype=bf16)
+    q_grad, error, term = call(
+        functools.partial(grad_kernel, grad_scale, last),
+        (shape(2 * tokens, bins, dtype=bf16), shape(tokens, bins), block),
+        *parts,
+        goal,
+        cols_turned,
+    )
+    arrived = [across(term, 2 * last)]
+    rest = tuple(range(last - 1, 0, -1))
+    *terms, owned = call(
+        functools.partial(term_kernel, rest + (0,)),
+        (*(block for _ in rest), shape(head_rows, bins)),
+        cols_turned,
+        q_grad,
+    )
+    arrived += [across(t, 2 * o) for o, t in zip(rest, terms)]
+    for a in arrived:
+        owned = owned + a.astype(f32)
+    td_error = error[:, 0]
+
+    rows = head_rows // mp_size
+
+    def rows_of(k):
+        return lax.dynamic_slice(owned, ((mp_at + k) % mp_size * rows, 0), (rows, bins))
+
+    piece = rows_of(0)
+    for k in range(1, mp_size):
+        piece = piece + shifted(rows_of(k).astype(bf16), k).astype(f32)
+    piece = piece.astype(bf16)
+    head_grad = jnp.zeros((head_rows, bins), f32)
+    for k in range(mp_size):
+        got = shifted(piece, k) if k else piece
+        at = (mp_at - k + mp_size) % mp_size * rows
+        head_grad = lax.dynamic_update_slice(head_grad, got.astype(f32), (at, 0))
+    return td_error, head_grad
+
+
 def solution(mesh):
     placed = (
         P(("dp", "mp"), None),
@@ -68,6 +358,8 @@
         P(("dp", "mp")),
         P(("dp", "mp")),
     )
+
+
     return jax.shard_map(
         body,
         mesh=mesh,

time: 173 us -> 77.5 us (0.45)
  waiting for transfers between devices: 128 us -> 27 us
  starting transfers between devices: 0.16 us -> 28.2 us
  Pallas kernels: 0 us -> 14.2 us
  between operations: 14.5 us -> 0.94 us
  blocking collectives: 11.8 us -> 0 us
  matrix products: 11.4 us -> 0 us
    reduce_scatter x1 -> x0, waiting for transfers between devices: 48.7 us -> none  [body(): lax.psum_scatter(lax.dot_general(columns, q_grad, (((0,), (0,)), ((), ())...]
    psum x1 -> x0, waiting for transfers between devices: 39.8 us -> none  [body(): head_grad = lax.psum(grad_owned, 'mp')]
    all_gather x2 -> x0, waiting for transfers between devices: 38.1 us -> none  [the longest x1 28 us: body(): lax.all_gather(target_head, 'dp', axis=0, tiled=True)]
    ppermute x0 -> x23, starting transfers between devices: none -> 28.2 us  [the longest x14 14.9 us: across(): return lax.ppermute(value, 'dp', [(i, i ^ mask) for i in range(count)])]
    ppermute x0 -> x23, waiting for transfers between devices: none -> 27 us  [the longest x14 19.2 us: across(): return lax.ppermute(value, 'dp', [(i, i ^ mask) for i in range(count)])]
    pallas_call x0 -> x11, Pallas kernels: none -> 14.2 us  [call(): pl.pallas_call(kernel, out_shape=outs, scratch_shapes=scratch, in_specs=[...]
    unnamed x1 -> x0, blocking collectives: 11.8 us -> none
    dot_general x3 -> x0, matrix products: 11.4 us -> none  [the longest x1 4.22 us: body(): jnp.dot(features, online_full, preferred_element_type=jnp.float32)]
  transfers between devices with their start and end apart: 4 -> 23, of which waited for: 4 -> 13; matrix products, arithmetic and copies ran while one was open for 5% -> 1% of each run, Pallas kernels for 0% -> 13%
where the time goes in v1:
time: 77.5 us; the launch traced here: 77.3 us
  starting transfers between devices  28.2 us (36%)
  waiting for transfers between devices  27 us (35%)
  Pallas kernels  14.2 us (18%)
  local copies, waits for them, and re-layouts  6.61 us (9%)
  between operations  0.94 us (1%)
    ppermute x14, waiting for transfers between devices, across(): return lax.ppermute(value, 'dp', [(i, i ^ mask) for i in range(count)])  19.2 us
    ppermute x14, starting transfers between devices, across(): return lax.ppermute(value, 'dp', [(i, i ^ mask) for i in range(count)])  14.9 us
    pallas_call x11, Pallas kernels, call(): pl.pallas_call(kernel, out_shape=outs, scratch_shapes=scratch, in_specs=[...  14.2 us
    ppermute x9, starting transfers between devices, shifted(): lax.ppermute(value, 'mp', [(i, (i + step) % count) for i in range(count)])  13.3 us
    ppermute x9, waiting for transfers between devices, shifted(): lax.ppermute(value, 'mp', [(i, (i + step) % count) for i in range(count)])  7.8 us
    unnamed x24, local copies, waits for them, and re-layouts  5.8 us
  transfers between devices with their start and end apart: 23, of which 13 were waited for; matrix products, arithmetic and copies ran while one was open for 1% of the time, Pallas kernels for 13%

profile of v1, /device:TPU:0, one launch (start us, length us, event | category | flops | bytes accessed | tf_op | source)
XLA Modules:
  0.0 77.3 jit_solution(8442301680873730337)
XLA Ops:
  0.7 0.1 pad_add_fusion.at_ref
  0.7 2.2 %copy-done = bf16[288,7168]{1,0:T(8,128)(2,1)S(1)} copy-done((bf16[288,7168]{1,0:T(8,128)(2,1)S(1)}, bf16[288,7168]{1,0:T(8,128)(2,1)}, u32[]{:S(2)}) %copy-start) | copy-done | bytes 4128792
  2.9 2.0 %shard_map.86 = bf16[4,288,896]{2,1,0:T(8,128)(2,1)} custom-call(s32[12]{0:T(128)S(1)} %pad_add_fusion.at_ref, bf16[288,7168]{1,0:T(8,128)(2,1)S(1)} %copy-done), custom_call_target="tpu_custom_call" | custom-call | tf_op jit(solution)/shard_map/pallas_call | solution.py:38
  5.0 0.5 collective-permute-start
  5.5 2.5 %collective-permute-start.1 = (bf16[896,128]{1,0:T(8,128)(2,1)S(1)}, bf16[896,128]{1,0:T(8,128)(2,1)S(1)}, u32[]{:S(2)}, u32[]{:S(2)}) collective-permute-start(bf16[896,128]{1,0:T(8,128)(2,1)S(1)} %copy-done.4), channel_id=1, source_target_pairs={{0,8},{4,12},{8,0},{12,4},{16,24},{20,28},{24,16},{28,20},{1,9},{5... | collective-permute-start | bytes 688136 | tf_op jit(solution)/shard_map/ppermute | solution.py:29
  7.9 1.5 %collective-permute-start.2 = (bf16[896,128]{1,0:T(8,128)(2,1)S(1)}, bf16[896,128]{1,0:T(8,128)(2,1)S(1)}, u32[]{:S(2)}, u32[]{:S(2)}) collective-permute-start(bf16[896,128]{1,0:T(8,128)(2,1)S(1)} %copy-done.4), channel_id=1, source_target_pairs={{0,16},{4,20},{8,24},{12,28},{16,0},{20,4},{24,8},{28,12},{1,17},{... | collective-permute-start | bytes 688136 | tf_op jit(solution)/shard_map/ppermute | solution.py:29
  9.5 0.5 collective-permute-start.7
  10.0 0.0 collective-permute-start.8
  10.0 4.4 %collective-permute-done.1.refs_0_.refs_1_ = bf16[896,128]{1,0:T(8,128)(2,1)S(1)} collective-permute-done((bf16[896,128]{1,0:T(8,128)(2,1)S(1)}, bf16[896,128]{1,0:T(8,128)(2,1)S(1)}, u32[]{:S(2)}, u32[]{:S(2)}) %collective-permute-start.1) | collective-permute-done | bytes 229408 | tf_op jit(solution)/shard_map/ppermute | solution.py:29
  14.4 3.0 %collective-permute-start.6 = (bf16[896,128]{1,0:T(8,128)(2,1)S(1)}, bf16[896,128]{1,0:T(8,128)(2,1)}, u32[]{:S(2)}, u32[]{:S(2)}) collective-permute-start(bf16[896,128]{1,0:T(8,128)(2,1)S(1)} %copy-done.3), channel_id=1, source_target_pairs={{0,24},{4,28},{8,16},{12,20},{16,8},{20,12},{24,0},{28,4},{1,25},{... | collective-permute-start | bytes 688136 | tf_op jit(solution)/shard_map/ppermute | solution.py:29
  17.4 0.0 collective-permute-done.2.refs_1_.refs_2_
  17.4 0.8 %shard_map.87 = (bf16[448,128]{1,0:T(8,128)(2,1)}, bf16[448,128]{1,0:T(8,128)(2,1)}, bf16[448,128]{1,0:T(8,128)(2,1)}, bf16[448,128]{1,0:T(8,128)(2,1)}) custom-call(bf16[896,128]{1,0:T(8,128)(2,1)S(1)} %collective-permute-done.1.refs_0_.refs_1_, bf16[896,128]{1,0:T(8,128)(2,1)S(1)} %collective-permute-done.2.refs_1_.refs_2_), custom_call_target="tpu_custom_call" | custom-call | tf_op jit(solution)/shard_map/pallas_call | solution.py:38
  18.2 0.6 collective-permute-start.3
  18.7 0.6 collective-permute-done.7.refs_1_
  19.3 2.0 %collective-permute-start.4 = (bf16[448,128]{1,0:T(8,128)(2,1)}, bf16[448,128]{1,0:T(8,128)(2,1)}, u32[]{:S(2)}, u32[]{:S(2)}) collective-permute-start(bf16[448,128]{1,0:T(8,128)(2,1)} %get-tuple-element.13), channel_id=1, source_target_pairs={{0,8},{4,12},{8,0},{12,4},{16,24},{20,28},{24,16},{28,20},{1,9},{5... | collective-permute-start | bytes 344072 | tf_op jit(solution)/shard_map/ppermute | solution.py:29
  21.3 4.9 %collective-permute-done.8.refs_2_ = bf16[896,128]{1,0:T(8,128)(2,1)S(1)} collective-permute-done((bf16[896,128]{1,0:T(8,128)(2,1)S(1)}, bf16[896,128]{1,0:T(8,128)(2,1)S(1)}, u32[]{:S(2)}, u32[]{:S(2)}) %collective-permute-start.8) | collective-permute-done | bytes 229408 | tf_op jit(solution)/shard_map/ppermute | solution.py:29
  26.2 2.2 %copy-done.1 = bf16[288,7168]{1,0:T(8,128)(2,1)S(1)} copy-done((bf16[288,7168]{1,0:T(8,128)(2,1)S(1)}, bf16[288,7168]{1,0:T(8,128)(2,1)}, u32[]{:S(2)}) %copy-start.1) | copy-done | bytes 4128792
  28.4 0.7 copy-done.6
  29.0 1.5 %shard_map.90.refs_1_ = f32[2,288,128]{2,1,0:T(8,128)S(1)} custom-call(s32[12]{0:T(128)S(1)} %copy-done.6, bf16[288,7168]{1,0:T(8,128)(2,1)S(1)} %copy-done.1, bf16[4,288,896]{2,1,0:T(8,128)(2,1)S(1)} %collective-permute-done.theirs_ref, bf16[896,128]{1,0:T(8,128)(2,1)S(1)} %copy-done.3, bf16[896,128]{1,0:T(8,128)(2,1)S(1)} %collective-permute-done.7.refs_1_, ...), custom_call_target="tpu_custom_call" | custom-call | tf_op jit(solution)/shard_map/pallas_call | solution.py:38
  30.6 0.0 collective-permute-done.6.refs_0_
  30.6 1.4 %shard_map.91.part_ref = f32[2,288,128]{2,1,0:T(8,128)S(1)} custom-call(s32[12]{0:T(128)S(1)} %copy-done.6, bf16[288,7168]{1,0:T(8,128)(2,1)S(1)} %copy-done.1, bf16[4,288,896]{2,1,0:T(8,128)(2,1)S(1)} %collective-permute-done.theirs_ref, bf16[896,128]{1,0:T(8,128)(2,1)} %collective-permute-done.6.refs_0_, f32[2,288,128]{2,1,0:T(8,128)S(1)} %shard_map.90.refs_1_), custom_call_target="tpu_custom_call" | custom-call | tf_op jit(solution)/shard_map/pallas_call | solution.py:38
  32.0 0.1 collective-permute-start.9
  32.0 1.5 %shard_map.88.refs_2_ = f32[2,288,128]{2,1,0:T(8,128)S(1)} custom-call(s32[12]{0:T(128)S(1)} %copy-done.6, bf16[288,7168]{1,0:T(8,128)(2,1)S(1)} %copy-done.1, bf16[4,288,896]{2,1,0:T(8,128)(2,1)S(1)} %collective-permute-done.theirs_ref, bf16[896,128]{1,0:T(8,128)(2,1)S(1)} %copy-done.4, bf16[896,128]{1,0:T(8,128)(2,1)S(1)} %collective-permute-done.1.refs_0_.refs_1_, ...), custom_call_target="tpu_custom_call" | custom-call | tf_op jit(solution)/shard_map/pallas_call | solution.py:38
  33.6 0.0 copy-start.9
  33.6 0.0 copy-start.10
  33.6 0.0 copy-start.11
  33.6 0.0 copy-start.8
  33.6 0.0 copy-start.2
  33.6 0.0 collective-permute-done.3.refs_0_
  33.6 1.5 %shard_map.89.part_ref = f32[2,288,128]{2,1,0:T(8,128)S(1)} custom-call(s32[12]{0:T(128)S(1)} %copy-done.6, bf16[288,7168]{1,0:T(8,128)(2,1)S(1)} %copy-done.1, bf16[4,288,896]{2,1,0:T(8,128)(2,1)S(1)} %collective-permute-done.theirs_ref, bf16[448,128]{1,0:T(8,128)(2,1)S(1)} %collective-permute-done.3.refs_0_, ...), custom_call_target="tpu_custom_call" | custom-call | tf_op jit(solution)/shard_map/pallas_call | solution.py:38
  35.2 0.6 collective-permute-start.5
  35.9 0.1 collective-permute-start.10
  36.0 0.0 collective-permute-done.9.other_ref
  36.0 0.2 shard_map.92
  36.1 1.6 %collective-permute-start.11 = (f32[2,128]{1,0:T(2,128)S(1)}, f32[2,128]{1,0:T(2,128)S(1)}, u32[]{:S(2)}, u32[]{:S(2)}) collective-permute-start(f32[2,128]{1,0:T(2,128)S(1)} %get-tuple-element.15.refs_0_), channel_id=1, source_target_pairs={{0,1},{1,2},{2,3},{3,0},{4,5},{5,6},{6,7},{7,4},{8,9},{9,10},{10,1... | collective-permute-start | bytes 3080 | tf_op jit(solution)/shard_map/ppermute | solution.py:34
  37.8 2.6 %collective-permute-start.12 = (f32[2,128]{1,0:T(2,128)S(1)}, f32[2,128]{1,0:T(2,128)S(1)}, u32[]{:S(2)}, u32[]{:S(2)}) collective-permute-start(f32[2,128]{1,0:T(2,128)S(1)} %get-tuple-element.15.refs_0_), channel_id=1, source_target_pairs={{0,2},{1,3},{2,0},{3,1},{4,6},{5,7},{6,4},{7,5},{8,10},{9,11},{10,... | collective-permute-start | bytes 3080 | tf_op jit(solution)/shard_map/ppermute | solution.py:34
  40.4 1.3 %collective-permute-start.13 = (f32[2,128]{1,0:T(2,128)S(1)}, f32[2,128]{1,0:T(2,128)S(1)}, u32[]{:S(2)}, u32[]{:S(2)}) collective-permute-start(f32[2,128]{1,0:T(2,128)S(1)} %get-tuple-element.15.refs_0_), channel_id=1, source_target_pairs={{0,3},{1,0},{2,1},{3,2},{4,7},{5,4},{6,5},{7,6},{8,11},{9,8},{10,9... | collective-permute-start | bytes 3080 | tf_op jit(solution)/shard_map/ppermute | solution.py:34
  41.7 1.8 %shard_map.94.cols_ref = bf16[4,896,576]{2,1,0:T(8,128)(2,1)S(1)} custom-call(s32[12]{0:T(128)S(1)} %copy-done.6, bf16[288,7168]{1,0:T(8,128)(2,1)S(1)} %copy-done.2, bf16[4,288,896]{2,1,0:T(8,128)(2,1)S(1)} %collective-permute-done.theirs_ref), custom_call_target="tpu_custom_call" | custom-call | tf_op jit(solution)/shard_map/pallas_call | solution.py:38
  43.5 0.4 collective-permute-done.13.refs_3_
  43.9 1.5 %shard_map.93.goal_ref = f32[2,288,128]{2,1,0:T(8,128)S(1)} custom-call(s32[12]{0:T(128)S(1)} %copy-done.6, f32[2,288,128]{2,1,0:T(8,128)S(1)} %get-tuple-element.14.best_ref, f32[4,288]{1,0:T(4,128)S(1)} %pad_maximum_fusion.scalar_ref, f32[4,288]{1,0:T(4,128)S(1)} %collective-permute-done.10.other_ref, f32[2,128]{1,0:T(2,128)S(1)} %get-tuple-element.15.refs_0_, ...), custom_call_target="tpu_custom_call" | custom-call | tf_op jit(solution)/shard_map/pallas_call | solution.py:38
  45.4 1.0 %shard_map.95 = (bf16[576,128]{1,0:T(8,128)(2,1)S(1)}, f32[288,128]{1,0:T(8,128)S(1)}, bf16[896,128]{1,0:T(8,128)(2,1)S(1)}) custom-call(f32[2,288,128]{2,1,0:T(8,128)S(1)} %shard_map.89.part_ref, f32[2,288,128]{2,1,0:T(8,128)S(1)} %collective-permute-done.5.other_ref, f32[2,288,128]{2,1,0:T(8,128)S(1)} %shard_map.93.goal_ref, ...), custom_call_target="tpu_custom_call" | custom-call | tf_op jit(solution)/shard_map/pallas_call | solution.py:38
  46.4 1.0 %shard_map.96 = (bf16[896,128]{1,0:T(8,128)(2,1)S(1)}, bf16[896,128]{1,0:T(8,128)(2,1)S(1)}, f32[896,128]{1,0:T(8,128)S(1)}) custom-call(bf16[4,896,576]{2,1,0:T(8,128)(2,1)S(1)} %shard_map.94.cols_ref, bf16[576,128]{1,0:T(8,128)(2,1)S(1)} %get-tuple-element.17.grad_ref), custom_call_target="tpu_custom_call" | custom-call | tf_op jit(solution)/shard_map/pallas_call | solution.py:38
  47.4 1.6 %collective-permute-start.15 = (bf16[896,128]{1,0:T(8,128)(2,1)S(1)}, bf16[896,128]{1,0:T(8,128)(2,1)S(1)}, u32[]{:S(2)}, u32[]{:S(2)}) collective-permute-start(bf16[896,128]{1,0:T(8,128)(2,1)S(1)} %get-tuple-element.20), channel_id=1, source_target_pairs={{0,16},{4,20},{8,24},{12,28},{16,0},{20,4},{24,8},{28,12},{1,17},{... | collective-permute-start | bytes 688136 | tf_op jit(solution)/shard_map/ppermute | solution.py:29
  49.0 0.5 collective-permute-start.16
  49.5 1.4 %collective-permute-start.14 = (bf16[896,128]{1,0:T(8,128)(2,1)S(1)}, bf16[896,128]{1,0:T(8,128)(2,1)S(1)}, u32[]{:S(2)}, u32[]{:S(2)}) collective-permute-start(bf16[896,128]{1,0:T(8,128)(2,1)S(1)} %get-tuple-element.19), channel_id=1, source_target_pairs={{0,24},{4,28},{8,16},{12,20},{16,8},{20,12},{24,0},{28,4},{1,25},{... | collective-permute-start | bytes 688136 | tf_op jit(solution)/shard_map/ppermute | solution.py:29
  51.0 4.1 %collective-permute-done.15 = bf16[896,128]{1,0:T(8,128)(2,1)S(1)} collective-permute-done((bf16[896,128]{1,0:T(8,128)(2,1)S(1)}, bf16[896,128]{1,0:T(8,128)(2,1)S(1)}, u32[]{:S(2)}, u32[]{:S(2)}) %collective-permute-start.15) | collective-permute-done | bytes 229408 | tf_op jit(solution)/shard_map/ppermute | solution.py:29
  55.0 2.4 %collective-permute-done.16 = bf16[896,128]{1,0:T(8,128)(2,1)S(1)} collective-permute-done((bf16[896,128]{1,0:T(8,128)(2,1)S(1)}, bf16[896,128]{1,0:T(8,128)(2,1)S(1)}, u32[]{:S(2)}, u32[]{:S(2)}) %collective-permute-start.16) | collective-permute-done | bytes 229408 | tf_op jit(solution)/shard_map/ppermute | solution.py:29
  57.5 2.9 %collective-permute-done.14 = bf16[896,128]{1,0:T(8,128)(2,1)S(1)} collective-permute-done((bf16[896,128]{1,0:T(8,128)(2,1)S(1)}, bf16[896,128]{1,0:T(8,128)(2,1)S(1)}, u32[]{:S(2)}, u32[]{:S(2)}) %collective-permute-start.14) | collective-permute-done | bytes 229408 | tf_op jit(solution)/shard_map/ppermute | solution.py:29
  60.3 0.1 convert_add_fusion
  60.5 0.7 collective-permute-start.17
  61.2 2.5 %collective-permute-start.18 = (bf16[224,128]{1,0:T(8,128)(2,1)S(1)}, bf16[224,128]{1,0:T(8,128)(2,1)S(1)}, u32[]{:S(2)}, u32[]{:S(2)}) collective-permute-start(bf16[224,128]{1,0:T(8,128)(2,1)S(1)} %get-tuple-element.26), channel_id=1, source_target_pairs={{0,2},{1,3},{2,0},{3,1},{4,6},{5,7},{6,4},{7,5},{8,10},{9,11},{10,... | collective-permute-start | bytes 172040 | tf_op jit(solution)/shard_map/ppermute | solution.py:34
  63.7 0.6 collective-permute-start.19
  64.4 2.2 %collective-permute-done.17 = bf16[224,128]{1,0:T(8,128)(2,1)S(1)} collective-permute-done((bf16[224,128]{1,0:T(8,128)(2,1)S(1)}, bf16[224,128]{1,0:T(8,128)(2,1)S(1)}, u32[]{:S(2)}, u32[]{:S(2)}) %collective-permute-start.17) | collective-permute-done | bytes 57376 | tf_op jit(solution)/shard_map/ppermute | solution.py:34
  66.6 0.9 %collective-permute-done.18 = bf16[224,128]{1,0:T(8,128)(2,1)S(1)} collective-permute-done((bf16[224,128]{1,0:T(8,128)(2,1)S(1)}, bf16[224,128]{1,0:T(8,128)(2,1)S(1)}, u32[]{:S(2)}, u32[]{:S(2)}) %collective-permute-start.18) | collective-permute-done | bytes 57376 | tf_op jit(solution)/shard_map/ppermute | solution.py:34
  67.5 0.6 collective-permute-done.19
  68.2 1.0 %collective-permute-start.20 = (bf16[224,128]{1,0:T(8,128)(2,1)S(1)}, bf16[224,128]{1,0:T(8,128)(2,1)S(1)}, u32[]{:S(2)}, u32[]{:S(2)}) collective-permute-start(bf16[224,128]{1,0:T(8,128)(2,1)S(1)} %get-tuple-element.23), channel_id=1, source_target_pairs={{0,1},{1,2},{2,3},{3,0},{4,5},{5,6},{6,7},{7,4},{8,9},{9,10},{10,1... | collective-permute-start | bytes 172040 | tf_op jit(solution)/shard_map/ppermute | solution.py:34
  69.2 0.7 slice_reduce_fusion
  70.0 2.4 %collective-permute-start.21 = (bf16[224,128]{1,0:T(8,128)(2,1)S(1)}, bf16[224,128]{1,0:T(8,128)(2,1)S(1)}, u32[]{:S(2)}, u32[]{:S(2)}) collective-permute-start(bf16[224,128]{1,0:T(8,128)(2,1)S(1)} %get-tuple-element.23), channel_id=1, source_target_pairs={{0,2},{1,3},{2,0},{3,1},{4,6},{5,7},{6,4},{7,5},{8,10},{9,11},{10,... | collective-permute-start | bytes 172040 | tf_op jit(solution)/shard_map/ppermute | solution.py:34
  72.3 0.5 collective-permute-start.22
  72.8 1.4 %collective-permute-done.20 = bf16[224,128]{1,0:T(8,128)(2,1)S(1)} collective-permute-done((bf16[224,128]{1,0:T(8,128)(2,1)S(1)}, bf16[224,128]{1,0:T(8,128)(2,1)S(1)}, u32[]{:S(2)}, u32[]{:S(2)}) %collective-permute-start.20) | collective-permute-done | bytes 57376 | tf_op jit(solution)/shard_map/ppermute | solution.py:34
  74.3 1.3 %collective-permute-done.21 = bf16[224,128]{1,0:T(8,128)(2,1)S(1)} collective-permute-done((bf16[224,128]{1,0:T(8,128)(2,1)S(1)}, bf16[224,128]{1,0:T(8,128)(2,1)S(1)}, u32[]{:S(2)}, u32[]{:S(2)}) %collective-permute-start.21) | collective-permute-done | bytes 57376 | tf_op jit(solution)/shard_map/ppermute | solution.py:34
  75.6 0.9 %collective-permute-done.22 = bf16[224,128]{1,0:T(8,128)(2,1)S(1)} collective-permute-done((bf16[224,128]{1,0:T(8,128)(2,1)S(1)}, bf16[224,128]{1,0:T(8,128)(2,1)S(1)}, u32[]{:S(2)}, u32[]{:S(2)}) %collective-permute-start.22) | collective-permute-done | bytes 57376 | tf_op jit(solution)/shard_map/ppermute | solution.py:34
  76.5 0.0 copy-start.7
  76.5 0.8 copy-done.7
  (36 shorter events, 0.2 us)
Async XLA Ops:
  0.7 2.2 %copy-start = (bf16[288,7168]{1,0:T(8,128)(2,1)S(1)}, bf16[288,7168]{1,0:T(8,128)(2,1)}, u32[]{:S(2)}) copy-start(bf16[288,7168]{1,0:T(8,128)(2,1)} %features_ref.11) | copy-start | bytes 12386308
  2.9 16.4 %copy-start.5 = (s32[12]{0:T(128)}, s32[12]{0:T(128)S(1)}, u32[]{:S(2)}) copy-start(s32[12]{0:T(128)S(1)} %pad_add_fusion.at_ref) | copy-start | bytes 148
  2.9 2.5 %copy-start.4 = (bf16[896,128]{1,0:T(8,128)(2,1)S(1)}, bf16[896,128]{1,0:T(8,128)(2,1)}, u32[]{:S(2)}) copy-start(bf16[896,128]{1,0:T(8,128)(2,1)} %refs_0_.2) | copy-start | bytes 688132
  2.9 6.5 %copy-start.3 = (bf16[896,128]{1,0:T(8,128)(2,1)S(1)}, bf16[896,128]{1,0:T(8,128)(2,1)}, u32[]{:S(2)}) copy-start(bf16[896,128]{1,0:T(8,128)(2,1)} %refs_0_.3) | copy-start | bytes 688132
  5.0 21.3 %collective-permute-start = (bf16[4,288,896]{2,1,0:T(8,128)(2,1)}, bf16[4,288,896]{2,1,0:T(8,128)(2,1)S(1)}, u32[]{:S(2)}, u32[]{:S(2)}) collective-permute-start(bf16[4,288,896]{2,1,0:T(8,128)(2,1)} %shard_map.86), channel_id=1, source_target_pairs={{0,4},{4,0},{8,12},{12,8},{16,20},{20,16},{24,28},{28,24},{1,5},{5... | collective-permute-start | bytes 6193160 | tf_op jit(solution)/shard_map/ppermute | solution.py:29
  5.5 8.9 %collective-permute-start.1 = (bf16[896,128]{1,0:T(8,128)(2,1)S(1)}, bf16[896,128]{1,0:T(8,128)(2,1)S(1)}, u32[]{:S(2)}, u32[]{:S(2)}) collective-permute-start(bf16[896,128]{1,0:T(8,128)(2,1)S(1)} %copy-done.4), channel_id=1, source_target_pairs={{0,8},{4,12},{8,0},{12,4},{16,24},{20,28},{24,16},{28,20},{1,9},{5... | collective-permute-start | bytes 688136 | tf_op jit(solution)/shard_map/ppermute | solution.py:29
  7.9 9.4 %collective-permute-start.2 = (bf16[896,128]{1,0:T(8,128)(2,1)S(1)}, bf16[896,128]{1,0:T(8,128)(2,1)S(1)}, u32[]{:S(2)}, u32[]{:S(2)}) collective-permute-start(bf16[896,128]{1,0:T(8,128)(2,1)S(1)} %copy-done.4), channel_id=1, source_target_pairs={{0,16},{4,20},{8,24},{12,28},{16,0},{20,4},{24,8},{28,12},{1,17},{... | collective-permute-start | bytes 688136 | tf_op jit(solution)/shard_map/ppermute | solution.py:29
  9.5 9.8 %collective-permute-start.7 = (bf16[896,128]{1,0:T(8,128)(2,1)S(1)}, bf16[896,128]{1,0:T(8,128)(2,1)S(1)}, u32[]{:S(2)}, u32[]{:S(2)}) collective-permute-start(bf16[896,128]{1,0:T(8,128)(2,1)S(1)} %copy-done.3), channel_id=1, source_target_pairs={{0,8},{4,12},{8,0},{12,4},{16,24},{20,28},{24,16},{28,20},{1,9},{5... | collective-permute-start | bytes 688136 | tf_op jit(solution)/shard_map/ppermute | solution.py:29
  10.0 16.2 %collective-permute-start.8 = (bf16[896,128]{1,0:T(8,128)(2,1)S(1)}, bf16[896,128]{1,0:T(8,128)(2,1)S(1)}, u32[]{:S(2)}, u32[]{:S(2)}) collective-permute-start(bf16[896,128]{1,0:T(8,128)(2,1)S(1)} %copy-done.3), channel_id=1, source_target_pairs={{0,16},{4,20},{8,24},{12,28},{16,0},{20,4},{24,8},{28,12},{1,17},{... | collective-permute-start | bytes 688136 | tf_op jit(solution)/shard_map/ppermute | solution.py:29
  14.4 16.2 %collective-permute-start.6 = (bf16[896,128]{1,0:T(8,128)(2,1)S(1)}, bf16[896,128]{1,0:T(8,128)(2,1)}, u32[]{:S(2)}, u32[]{:S(2)}) collective-permute-start(bf16[896,128]{1,0:T(8,128)(2,1)S(1)} %copy-done.3), channel_id=1, source_target_pairs={{0,24},{4,28},{8,16},{12,20},{16,8},{20,12},{24,0},{28,4},{1,25},{... | collective-permute-start | bytes 688136 | tf_op jit(solution)/shard_map/ppermute | solution.py:29
  18.2 15.5 %collective-permute-start.3 = (bf16[448,128]{1,0:T(8,128)(2,1)}, bf16[448,128]{1,0:T(8,128)(2,1)S(1)}, u32[]{:S(2)}, u32[]{:S(2)}) collective-permute-start(bf16[448,128]{1,0:T(8,128)(2,1)} %get-tuple-element.12), channel_id=1, source_target_pairs={{0,16},{4,20},{8,24},{12,28},{16,0},{20,4},{24,8},{28,12},{1,17},{... | collective-permute-start | bytes 344072 | tf_op jit(solution)/shard_map/ppermute | solution.py:29
  19.3 14.3 %collective-permute-start.4 = (bf16[448,128]{1,0:T(8,128)(2,1)}, bf16[448,128]{1,0:T(8,128)(2,1)}, u32[]{:S(2)}, u32[]{:S(2)}) collective-permute-start(bf16[448,128]{1,0:T(8,128)(2,1)} %get-tuple-element.13), channel_id=1, source_target_pairs={{0,8},{4,12},{8,0},{12,4},{16,24},{20,28},{24,16},{28,20},{1,9},{5... | collective-permute-start | bytes 344072 | tf_op jit(solution)/shard_map/ppermute | solution.py:29
  26.2 2.2 %copy-start.1 = (bf16[288,7168]{1,0:T(8,128)(2,1)S(1)}, bf16[288,7168]{1,0:T(8,128)(2,1)}, u32[]{:S(2)}) copy-start(bf16[288,7168]{1,0:T(8,128)(2,1)} %features_ref.11) | copy-start | bytes 12386308
  28.4 0.7 copy-start.6
  32.0 4.0 %collective-permute-start.9 = (f32[2,288,128]{2,1,0:T(8,128)S(1)}, f32[2,288,128]{2,1,0:T(8,128)S(1)}, u32[]{:S(2)}, u32[]{:S(2)}) collective-permute-start(f32[2,288,128]{2,1,0:T(8,128)S(1)} %shard_map.91.part_ref), channel_id=1, source_target_pairs={{0,4},{4,0},{8,12},{12,8},{16,20},{20,16},{24,28},{28,24},{1,5},{5... | collective-permute-start | bytes 884744 | tf_op jit(solution)/shard_map/ppermute | solution.py:29
  33.6 2.2 %copy-start.9 = (s32[288]{0:T(512)S(1)}, s32[288]{0:T(512)}, u32[]{:S(2)}) copy-start(s32[288]{0:T(512)} %param.11) | copy-start | bytes 3460
  33.6 2.2 %copy-start.10 = (s32[288]{0:T(512)S(1)}, s32[288]{0:T(512)}, u32[]{:S(2)}) copy-start(s32[288]{0:T(512)} %param.10) | copy-start | bytes 3460
  33.6 2.2 %copy-start.11 = (s32[288]{0:T(512)S(1)}, s32[288]{0:T(512)}, u32[]{:S(2)}) copy-start(s32[288]{0:T(512)} %param.13) | copy-start | bytes 3460
  33.6 2.2 %copy-start.8 = (f32[288]{0:T(512)S(1)}, f32[288]{0:T(512)}, u32[]{:S(2)}) copy-start(f32[288]{0:T(512)} %param.12) | copy-start | bytes 3460
  33.6 8.1 %copy-start.2 = (bf16[288,7168]{1,0:T(8,128)(2,1)S(1)}, bf16[288,7168]{1,0:T(8,128)(2,1)}, u32[]{:S(2)}) copy-start(bf16[288,7168]{1,0:T(8,128)(2,1)} %features_ref.11) | copy-start | bytes 12386308
  35.2 10.2 %collective-permute-start.5 = (f32[2,288,128]{2,1,0:T(8,128)S(1)}, f32[2,288,128]{2,1,0:T(8,128)S(1)}, u32[]{:S(2)}, u32[]{:S(2)}) collective-permute-start(f32[2,288,128]{2,1,0:T(8,128)S(1)} %shard_map.89.part_ref), channel_id=1, source_target_pairs={{0,4},{4,0},{8,12},{12,8},{16,20},{20,16},{24,28},{28,24},{1,5},{5... | collective-permute-start | bytes 884744 | tf_op jit(solution)/shard_map/ppermute | solution.py:29
  35.9 7.6 %collective-permute-start.10 = (f32[4,288]{1,0:T(4,128)S(1)}, f32[4,288]{1,0:T(4,128)S(1)}, u32[]{:S(2)}, u32[]{:S(2)}) collective-permute-start(f32[4,288]{1,0:T(4,128)S(1)} %pad_maximum_fusion.scalar_ref), channel_id=1, source_target_pairs={{0,4},{4,0},{8,12},{12,8},{16,20},{20,16},{24,28},{28,24},{1,5},{5... | collective-permute-start | bytes 13832 | tf_op jit(solution)/shard_map/ppermute | solution.py:29
  36.1 7.4 %collective-permute-start.11 = (f32[2,128]{1,0:T(2,128)S(1)}, f32[2,128]{1,0:T(2,128)S(1)}, u32[]{:S(2)}, u32[]{:S(2)}) collective-permute-start(f32[2,128]{1,0:T(2,128)S(1)} %get-tuple-element.15.refs_0_), channel_id=1, source_target_pairs={{0,1},{1,2},{2,3},{3,0},{4,5},{5,6},{6,7},{7,4},{8,9},{9,10},{10,1... | collective-permute-start | bytes 3080 | tf_op jit(solution)/shard_map/ppermute | solution.py:34
  37.8 5.8 %collective-permute-start.12 = (f32[2,128]{1,0:T(2,128)S(1)}, f32[2,128]{1,0:T(2,128)S(1)}, u32[]{:S(2)}, u32[]{:S(2)}) collective-permute-start(f32[2,128]{1,0:T(2,128)S(1)} %get-tuple-element.15.refs_0_), channel_id=1, source_target_pairs={{0,2},{1,3},{2,0},{3,1},{4,6},{5,7},{6,4},{7,5},{8,10},{9,11},{10,... | collective-permute-start | bytes 3080 | tf_op jit(solution)/shard_map/ppermute | solution.py:34
  40.4 3.6 %collective-permute-start.13 = (f32[2,128]{1,0:T(2,128)S(1)}, f32[2,128]{1,0:T(2,128)S(1)}, u32[]{:S(2)}, u32[]{:S(2)}) collective-permute-start(f32[2,128]{1,0:T(2,128)S(1)} %get-tuple-element.15.refs_0_), channel_id=1, source_target_pairs={{0,3},{1,0},{2,1},{3,2},{4,7},{5,4},{6,5},{7,6},{8,11},{9,8},{10,9... | collective-permute-start | bytes 3080 | tf_op jit(solution)/shard_map/ppermute | solution.py:34
  47.4 7.6 %collective-permute-start.15 = (bf16[896,128]{1,0:T(8,128)(2,1)S(1)}, bf16[896,128]{1,0:T(8,128)(2,1)S(1)}, u32[]{:S(2)}, u32[]{:S(2)}) collective-permute-start(bf16[896,128]{1,0:T(8,128)(2,1)S(1)} %get-tuple-element.20), channel_id=1, source_target_pairs={{0,16},{4,20},{8,24},{12,28},{16,0},{20,4},{24,8},{28,12},{1,17},{... | collective-permute-start | bytes 688136 | tf_op jit(solution)/shard_map/ppermute | solution.py:29
  49.0 8.5 %collective-permute-start.16 = (bf16[896,128]{1,0:T(8,128)(2,1)S(1)}, bf16[896,128]{1,0:T(8,128)(2,1)S(1)}, u32[]{:S(2)}, u32[]{:S(2)}) collective-permute-start(bf16[896,128]{1,0:T(8,128)(2,1)S(1)} %get-tuple-element.21), channel_id=1, source_target_pairs={{0,8},{4,12},{8,0},{12,4},{16,24},{20,28},{24,16},{28,20},{1,9},{5... | collective-permute-start | bytes 688136 | tf_op jit(solution)/shard_map/ppermute | solution.py:29
  49.5 10.8 %collective-permute-start.14 = (bf16[896,128]{1,0:T(8,128)(2,1)S(1)}, bf16[896,128]{1,0:T(8,128)(2,1)S(1)}, u32[]{:S(2)}, u32[]{:S(2)}) collective-permute-start(bf16[896,128]{1,0:T(8,128)(2,1)S(1)} %get-tuple-element.19), channel_id=1, source_target_pairs={{0,24},{4,28},{8,16},{12,20},{16,8},{20,12},{24,0},{28,4},{1,25},{... | collective-permute-start | bytes 688136 | tf_op jit(solution)/shard_map/ppermute | solution.py:29
  60.5 6.1 %collective-permute-start.17 = (bf16[224,128]{1,0:T(8,128)(2,1)S(1)}, bf16[224,128]{1,0:T(8,128)(2,1)S(1)}, u32[]{:S(2)}, u32[]{:S(2)}) collective-permute-start(bf16[224,128]{1,0:T(8,128)(2,1)S(1)} %get-tuple-element.24), channel_id=1, source_target_pairs={{0,1},{1,2},{2,3},{3,0},{4,5},{5,6},{6,7},{7,4},{8,9},{9,10},{10,1... | collective-permute-start | bytes 172040 | tf_op jit(solution)/shard_map/ppermute | solution.py:34
  61.2 6.3 %collective-permute-start.18 = (bf16[224,128]{1,0:T(8,128)(2,1)S(1)}, bf16[224,128]{1,0:T(8,128)(2,1)S(1)}, u32[]{:S(2)}, u32[]{:S(2)}) collective-permute-start(bf16[224,128]{1,0:T(8,128)(2,1)S(1)} %get-tuple-element.26), channel_id=1, source_target_pairs={{0,2},{1,3},{2,0},{3,1},{4,6},{5,7},{6,4},{7,5},{8,10},{9,11},{10,... | collective-permute-start | bytes 172040 | tf_op jit(solution)/shard_map/ppermute | solution.py:34
  63.7 4.4 %collective-permute-start.19 = (bf16[224,128]{1,0:T(8,128)(2,1)S(1)}, bf16[224,128]{1,0:T(8,128)(2,1)S(1)}, u32[]{:S(2)}, u32[]{:S(2)}) collective-permute-start(bf16[224,128]{1,0:T(8,128)(2,1)S(1)} %get-tuple-element.25), channel_id=1, source_target_pairs={{0,3},{1,0},{2,1},{3,2},{4,7},{5,4},{6,5},{7,6},{8,11},{9,8},{10,9... | collective-permute-start | bytes 172040 | tf_op jit(solution)/shard_map/ppermute | solution.py:34
  68.2 6.0 %collective-permute-start.20 = (bf16[224,128]{1,0:T(8,128)(2,1)S(1)}, bf16[224,128]{1,0:T(8,128)(2,1)S(1)}, u32[]{:S(2)}, u32[]{:S(2)}) collective-permute-start(bf16[224,128]{1,0:T(8,128)(2,1)S(1)} %get-tuple-element.23), channel_id=1, source_target_pairs={{0,1},{1,2},{2,3},{3,0},{4,5},{5,6},{6,7},{7,4},{8,9},{9,10},{10,1... | collective-permute-start | bytes 172040 | tf_op jit(solution)/shard_map/ppermute | solution.py:34
  70.0 5.6 %collective-permute-start.21 = (bf16[224,128]{1,0:T(8,128)(2,1)S(1)}, bf16[224,128]{1,0:T(8,128)(2,1)S(1)}, u32[]{:S(2)}, u32[]{:S(2)}) collective-permute-start(bf16[224,128]{1,0:T(8,128)(2,1)S(1)} %get-tuple-element.23), channel_id=1, source_target_pairs={{0,2},{1,3},{2,0},{3,1},{4,6},{5,7},{6,4},{7,5},{8,10},{9,11},{10,... | collective-permute-start | bytes 172040 | tf_op jit(solution)/shard_map/ppermute | solution.py:34
  72.3 4.2 %collective-permute-start.22 = (bf16[224,128]{1,0:T(8,128)(2,1)S(1)}, bf16[224,128]{1,0:T(8,128)(2,1)S(1)}, u32[]{:S(2)}, u32[]{:S(2)}) collective-permute-start(bf16[224,128]{1,0:T(8,128)(2,1)S(1)} %get-tuple-element.23), channel_id=1, source_target_pairs={{0,3},{1,0},{2,1},{3,2},{4,7},{5,4},{6,5},{7,6},{8,11},{9,8},{10,9... | collective-permute-start | bytes 172040 | tf_op jit(solution)/shard_map/ppermute | solution.py:34
  76.5 0.8 copy-start.7

commit v2 on v1

--- a/solution.py
+++ b/solution.py
@@ -29,9 +29,9 @@
     return lax.ppermute(value, "dp", [(i, i ^ mask) for i in range(count)])
 
 
-def shifted(value, step):
+def mixed(value, mask):
     count = lax.axis_size("mp")
-    return lax.ppermute(value, "mp", [(i, (i + step) % count) for i in range(count)])
+    return lax.ppermute(value, "mp", [(i, i ^ mask) for i in range(count)])
 
 
 def call(kernel, outs, *args, smem=0, scratch=()):
@@ -61,59 +61,42 @@
     return {0: (shard,), **{o: (across(shard, 2 * o),) for o in relay_order(chips)}}
 
 
-def first_hops(shard, chips):
-    return {o: (across(shard, 2 * o),) for o in relay_order(chips) if o & (o - 1) == 0}
-
-
-def halves_kernel(*refs):
-    count = len(refs) // 3
-    for ref, first_ref, second_ref in zip(refs[:count], refs[count::2], refs[count + 1 :: 2]):
-        half = first_ref.shape[0]
-        first_ref[...] = ref[:half]
-        second_ref[...] = ref[half:]
-
-
-def relayed(shard, held, chips):
-    half = shape(shard.shape[0] // 2, shard.shape[1], dtype=shard.dtype)
-    hops = [h[0] for h in held.values()]
-    parts = call(halves_kernel, (half,) * (2 * len(hops)), *hops)
-    split = dict(zip(held, zip(parts[::2], parts[1::2])))
-    held = {0: (shard,), **held}
-    for offset in relay_order(chips):
-        if offset in held:
-            continue
-        low = offset & -offset
-        high = 1 << (offset.bit_length() - 1)
-        first = split.get(offset ^ high, held[offset ^ high])[0]
-        second = split.get(offset ^ low, held[offset ^ low])[1]
-        held[offset] = (across(first, 2 * high), across(second, 2 * low))
-    return held
-
-
 def column(ref, at_ref, offset, width):
     return ref.at[:, pl.ds(pl.multiple_of(at_ref[offset] * width, width), width)]
 
 
-def cut_kernel(at_ref, features_ref, sent_ref):
-    chips, _, width = sent_ref.shape
+def load_kernel(features_ref, out_ref, sem):
+    copy = pltpu.make_async_copy(features_ref, out_ref, sem)
+    copy.start()
+    copy.wait()
+
+
+def loaded(features):
+    return pl.pallas_call(
+        load_kernel,
+        out_shape=shape(*features.shape, dtype=features.dtype),
+        in_specs=[ANY],
+        out_specs=VMEM,
+        scratch_shapes=[pltpu.SemaphoreType.DMA],
+        compiler_params=pltpu.CompilerParams(vmem_limit_bytes=16 * MIB),
+        name="load",
+    )(pltpu.with_memory_space_constraint(features, pltpu.HBM))
+
+
+def turn_kernel(at_ref, features_ref, theirs_ref, out_ref):
+    chips, width, _ = out_ref.shape
     for j in range(chips):
-        sent_ref[j] = column(features_ref, at_ref, chips + j, width)[...]
-
-
-def turn_kernel(at_ref, features_ref, theirs_ref, out_ref):
-    for j in range(theirs_ref.shape[0]):
-        mine = column(features_ref, at_ref, j, theirs_ref.shape[2])[...]
-        both = jnp.concatenate([mine, theirs_ref[j]], axis=0)
+        both = [column(ref, at_ref, j, width)[...] for ref in (features_ref, theirs_ref)]
+        both = jnp.concatenate(both, axis=0)
         out_ref[j] = both.T
 
 
-def logits_kernel(offsets, has_start, at_ref, features_ref, theirs_ref, *refs):
+def logits_kernel(width, offsets, has_start, at_ref, features_ref, theirs_ref, *refs):
     pieces, out_ref = refs[: len(offsets)], refs[-1]
-    width = theirs_ref.shape[2]
-    for side in range(2):
+    for side, ref in enumerate((features_ref, theirs_ref)):
         total = refs[-2][side] if has_start else None
         for (offset, at), piece in zip(offsets, pieces):
-            cols = (theirs_ref.at[offset], column(features_ref, at_ref, offset, width))[1 - side]
+            cols = column(ref, at_ref, offset, width)
             part = jnp.dot(
                 cols[:, at : at + piece.shape[0]], piece[...], preferred_element_type=f32
             )
@@ -121,7 +104,7 @@
         out_ref[side] = total
 
 
-def partial_logits(at, features, theirs, held, start=None):
+def partial_logits(width, at, features, theirs, held, start=None):
     offsets, pieces = [], []
     for offset, parts in held.items():
         row = 0
@@ -131,7 +114,7 @@
             row += part.shape[0]
     out = shape(2, features.shape[0], pieces[0].shape[1])
     extra = () if start is None else (start,)
-    kernel = functools.partial(logits_kernel, tuple(offsets), start is not None)
+    kernel = functools.partial(logits_kernel, width, tuple(offsets), start is not None)
     return call(kernel, out, at, features, theirs, *pieces, *extra, smem=1)
 
 
@@ -145,6 +128,12 @@
         best_ref[side] = jnp.broadcast_to(best, best_ref.shape[1:])
         picked = jnp.where(token == ADIM * lane, best, 0.0)
         firsts_ref[side : side + 1] = jnp.sum(picked, axis=0, keepdims=True)
+
+
+def join_kernel(first_ref, second_ref, out_ref):
+    rows = first_ref.shape[0]
+    out_ref[:rows] = first_ref[...]
+    out_ref[rows:] = second_ref[...]
 
 
 def goal_kernel(sources_at, at_ref, best_ref, scalar_ref, other_ref, *refs):
@@ -163,12 +152,14 @@
         action, nxt, rew, term = (
             columns[:tokens, 4 * side + i : 4 * side + i + 1] for i in range(4)
         )
-        step_at = nxt.astype(jnp.int32) >> (ADIM.bit_length() - 1)
+        local = nxt.astype(jnp.int32) - at_ref[at_ref.shape[0] - 2 + side]
+        step_at = local >> (ADIM.bit_length() - 1)
         jumped = jnp.zeros((tokens, lanes), f32)
-        for k, table in enumerate(firsts):
+        tables = [t[i : i + 1] for t in firsts for i in range(side, t.shape[0], 2)]
+        for k, table in enumerate(tables):
             label = lane + at_ref[sources_at + k] * steps
             hit = (label == step_at) & (lane < steps)
-            jumped = jnp.where(hit, table[side : side + 1], jumped)
+            jumped = jnp.where(hit, table, jumped)
         jumped = jnp.sum(jumped, axis=1, keepdims=True)
         following = pltpu.roll(best_ref[side], tokens - 1, 0)[:, :1]
         bootstrap = rew + DISCOUNT * (1.0 - term) * jumped
@@ -252,7 +243,8 @@
     head_rows, bins = online_head.shape
     mp_size = lax.axis_size("mp")
     dp_size = lax.axis_size("dp")
-    if head_rows % LANES or head_rows % (16 * mp_size) or dp_size & (dp_size - 1):
+    odd = dp_size & (dp_size - 1) or mp_size & (mp_size - 1)
+    if odd or head_rows % LANES or head_rows % (16 * mp_size):
         return plain_body(
             features, online_head, target_head, action_bin, next_index, reward, terminal
         )
@@ -263,48 +255,50 @@
     mp_at = lax.axis_index("mp")
     core, chip = dp_at & 1, dp_at >> 1
 
+    offset = jnp.arange(chips, dtype=jnp.int32)
+    owner = 2 * (chip ^ offset) + core
+    sources = mp_at ^ jnp.arange(mp_size, dtype=jnp.int32)
+    groups = (dp_at ^ jnp.arange(2, dtype=jnp.int32)) * group_size
+    at = jnp.concatenate([owner, sources, groups])
     target_held = direct_hops(target_head, chips)
-    online_hops = first_hops(online_head, chips)
-
-    offset = jnp.arange(chips, dtype=jnp.int32)
-    owner = 2 * (chip ^ offset)
-    at, other_at = owner + core, owner + 1 - core
-    sources = mp_at - jnp.arange(mp_size, dtype=jnp.int32)
-    sources = jnp.where(sources < 0, sources + mp_size, sources)
-    at = jnp.concatenate([at, other_at, sources])
-    block = shape(chips, tokens, head_rows, dtype=features.dtype)
-    sent = call(cut_kernel, block, at, features, smem=1)
-    theirs = across(sent, 1)
+    theirs = across(features, 1)
+    online_held = direct_hops(online_head, chips)
+
     scalars = jnp.stack(
         [
             action_bin.astype(f32),
-            (next_index - dp_at * group_size).astype(f32),
+            next_index.astype(f32),
             reward,
             terminal.astype(f32),
         ]
     )
     scalars = (scalars, across(scalars, 1))
+    features = loaded(features)
     out = shape(chips, head_rows, 2 * tokens, dtype=features.dtype)
     cols_turned = call(turn_kernel, out, at, features, theirs, smem=1)
-    online_held = relayed(online_head, online_hops, chips)
 
     last = chips - 1
     both = shape(2, tokens, bins)
 
     def logits(held):
-        early = {o: p for o, p in held.items() if o != last}
-        part = partial_logits(at, features, theirs, early)
-        part = partial_logits(at, features, theirs, {last: held[last]}, part)
+        early = {o: p for o, p in held.items() if o < chips // 2}
+        late = {o: p for o, p in held.items() if o not in early}
+        part = partial_logits(head_rows, at, features, theirs, early)
+        part = partial_logits(head_rows, at, features, theirs, late, part)
         return part, across(part, 1)
 
     parts = logits(target_held)
     lanes = -(-(tokens // ADIM) // LANES) * LANES
     best, firsts = call(best_kernel, (both, shape(2, lanes)), *parts)
-    tables = [firsts]
-    for k in range(1, mp_size):
-        tables.append(shifted(firsts, k))
+    tables, mask = [firsts], 1
+    while mask < mp_size:
+        if mask > 1:
+            out = shape(2 * mask, lanes)
+            tables = [call(join_kernel, out, *tables)]
+        tables.append(mixed(tables[0], mask))
+        mask *= 2
     goal = call(
-        functools.partial(goal_kernel, 2 * chips), both, at, best, *scalars, *tables, smem=1,
+        functools.partial(goal_kernel, chips), both, at, best, *scalars, *tables, smem=1,
         scratch=[pltpu.VMEM((8, -(-tokens // LANES) * LANES), f32)],
     )
 
@@ -334,17 +328,18 @@
     rows = head_rows // mp_size
 
     def rows_of(k):
-        return lax.dynamic_slice(owned, ((mp_at + k) % mp_size * rows, 0), (rows, bins))
-
+        return lax.dynamic_slice(owned, ((mp_at ^ k) * rows, 0), (rows, bins))
+
+    order = sorted(range(1, mp_size), key=lambda k: -(k >> 1))
     piece = rows_of(0)
-    for k in range(1, mp_size):
-        piece = piece + shifted(rows_of(k).astype(bf16), k).astype(f32)
+    for k in order:
+        got = mixed(rows_of(k).astype(bf16), k)
+        piece = piece + got.astype(f32)
     piece = piece.astype(bf16)
     head_grad = jnp.zeros((head_rows, bins), f32)
-    for k in range(mp_size):
-        got = shifted(piece, k) if k else piece
-        at = (mp_at - k + mp_size) % mp_size * rows
-        head_grad = lax.dynamic_update_slice(head_grad, got.astype(f32), (at, 0))
+    for k in [0] + order:
+        got = mixed(piece, k) if k else piece
+        head_grad = lax.dynamic_update_slice(head_grad, got.astype(f32), ((mp_at ^ k) * rows, 0))
     return td_error, head_grad
 
 

time: 77.5 us -> 77.2 us (level)
  Pallas kernels: 14.2 us -> 21.1 us
  waiting for transfers between devices: 27 us -> 22.7 us
  starting transfers between devices: 28.2 us -> 26.2 us
  local copies, waits for them, and re-layouts: 6.61 us -> 5.78 us
    ppermute x14 -> x13, waiting for transfers between devices: 19.2 us -> 12.4 us  [across(): return lax.ppermute(value, 'dp', [(i, i ^ mask) for i in range(count)])]
    pallas_call x11 -> x10, Pallas kernels: 14.2 us -> 18.8 us  [call(): pl.pallas_call(kernel, out_shape=outs, scratch_shapes=scratch, in_specs=[...]
    ppermute x9 -> x8, waiting for transfers between devices: 7.8 us -> 10.3 us  [mixed(): return lax.ppermute(value, 'mp', [(i, i ^ mask) for i in range(count)])]
    pallas_call x0 -> x1, Pallas kernels: none -> 2.22 us  [loaded(): pl.pallas_call(load_kernel, out_shape=shape(*features.shape, dtype=featur...]
    ppermute x9 -> x8, starting transfers between devices: 13.3 us -> 11.9 us  [mixed(): return lax.ppermute(value, 'mp', [(i, i ^ mask) for i in range(count)])]
    unnamed x24 -> x20, local copies, waits for them, and re-layouts: 5.8 us -> 4.97 us
    ppermute x14 -> x13, starting transfers between devices: 14.9 us -> 14.4 us  [across(): return lax.ppermute(value, 'dp', [(i, i ^ mask) for i in range(count)])]
  transfers between devices with their start and end apart: 23 -> 21, of which waited for: 13 -> 11; matrix products, arithmetic and copies ran while one was open for 1% -> 1% of each run, Pallas kernels for 13% -> 25%
where the time goes in v2:
time: 77.2 us; the launch traced here: 77 us
  starting transfers between devices  26.2 us (34%)
  waiting for transfers between devices  22.7 us (29%)
  Pallas kernels  21.1 us (27%)
  local copies, waits for them, and re-layouts  5.78 us (7%)
  between operations  0.95 us (1%)
    pallas_call x10, Pallas kernels, call(): pl.pallas_call(kernel, out_shape=outs, scratch_shapes=scratch, in_specs=[...  18.8 us
    ppermute x13, starting transfers between devices, across(): return lax.ppermute(value, 'dp', [(i, i ^ mask) for i in range(count)])  14.4 us
    ppermute x13, waiting for transfers between devices, across(): return lax.ppermute(value, 'dp', [(i, i ^ mask) for i in range(count)])  12.4 us
    ppermute x8, starting transfers between devices, mixed(): return lax.ppermute(value, 'mp', [(i, i ^ mask) for i in range(count)])  11.9 us
    ppermute x8, waiting for transfers between devices, mixed(): return lax.ppermute(value, 'mp', [(i, i ^ mask) for i in range(count)])  10.3 us
    unnamed x20, local copies, waits for them, and re-layouts  4.97 us
    pallas_call x1, Pallas kernels, loaded(): pl.pallas_call(load_kernel, out_shape=shape(*features.shape, dtype=featur...  2.22 us
  transfers between devices with their start and end apart: 21, of which 11 were waited for; matrix products, arithmetic and copies ran while one was open for 1% of the time, Pallas kernels for 25%

profile of v2, /device:TPU:0, one launch (start us, length us, event | category | flops | bytes accessed | tf_op | source)
XLA Modules:
  0.0 77.0 jit_solution(533146821683940192)
XLA Ops:
  0.6 0.6 collective-permute-start
  1.2 2.6 %collective-permute-start.7 = (bf16[896,128]{1,0:T(8,128)(2,1)}, bf16[896,128]{1,0:T(8,128)(2,1)S(1)}, u32[]{:S(2)}, u32[]{:S(2)}) collective-permute-start(bf16[896,128]{1,0:T(8,128)(2,1)} %refs_0_.3), channel_id=1, source_target_pairs={{0,8},{4,12},{8,0},{12,4},{16,24},{20,28},{24,16},{28,20},{1,9},{5... | collective-permute-start | bytes 688136 | tf_op jit(solution)/shard_map/ppermute | solution.py:29
  3.7 1.5 %collective-permute-start.5 = (bf16[896,128]{1,0:T(8,128)(2,1)}, bf16[896,128]{1,0:T(8,128)(2,1)S(1)}, u32[]{:S(2)}, u32[]{:S(2)}) collective-permute-start(bf16[896,128]{1,0:T(8,128)(2,1)} %refs_0_.3), channel_id=1, source_target_pairs={{0,16},{4,20},{8,24},{12,28},{16,0},{20,4},{24,8},{28,12},{1,17},{... | collective-permute-start | bytes 688136 | tf_op jit(solution)/shard_map/ppermute | solution.py:29
  5.3 0.0 collective-permute-start.6
  5.3 1.9 %collective-permute-start.3 = (bf16[896,128]{1,0:T(8,128)(2,1)}, bf16[896,128]{1,0:T(8,128)(2,1)S(1)}, u32[]{:S(2)}, u32[]{:S(2)}) collective-permute-start(bf16[896,128]{1,0:T(8,128)(2,1)} %refs_0_.2), channel_id=1, source_target_pairs={{0,8},{4,12},{8,0},{12,4},{16,24},{20,28},{24,16},{28,20},{1,9},{5... | collective-permute-start | bytes 688136 | tf_op jit(solution)/shard_map/ppermute | solution.py:29
  7.2 3.2 %collective-permute-done.7.refs_1_ = bf16[896,128]{1,0:T(8,128)(2,1)S(1)} collective-permute-done((bf16[896,128]{1,0:T(8,128)(2,1)}, bf16[896,128]{1,0:T(8,128)(2,1)S(1)}, u32[]{:S(2)}, u32[]{:S(2)}) %collective-permute-start.7) | collective-permute-done | bytes 229408 | tf_op jit(solution)/shard_map/ppermute | solution.py:29
  10.4 2.0 %collective-permute-start.1 = (bf16[896,128]{1,0:T(8,128)(2,1)}, bf16[896,128]{1,0:T(8,128)(2,1)S(1)}, u32[]{:S(2)}, u32[]{:S(2)}) collective-permute-start(bf16[896,128]{1,0:T(8,128)(2,1)} %refs_0_.2), channel_id=1, source_target_pairs={{0,16},{4,20},{8,24},{12,28},{16,0},{20,4},{24,8},{28,12},{1,17},{... | collective-permute-start | bytes 688136 | tf_op jit(solution)/shard_map/ppermute | solution.py:29
  12.5 0.0 collective-permute-done.theirs_ref
  12.5 1.4 %collective-permute-start.2 = (bf16[896,128]{1,0:T(8,128)(2,1)}, bf16[896,128]{1,0:T(8,128)(2,1)S(1)}, u32[]{:S(2)}, u32[]{:S(2)}) collective-permute-start(bf16[896,128]{1,0:T(8,128)(2,1)} %refs_0_.2), channel_id=1, source_target_pairs={{0,24},{4,28},{8,16},{12,20},{16,8},{20,12},{24,0},{28,4},{1,25},{... | collective-permute-start | bytes 688136 | tf_op jit(solution)/shard_map/ppermute | solution.py:29
  13.9 2.2 %load.1.features_ref = bf16[288,7168]{1,0:T(8,128)(2,1)S(1)} custom-call(bf16[288,7168]{1,0:T(8,128)(2,1)} %features_ref.1), custom_call_target="tpu_custom_call" | custom-call | tf_op jit(solution)/shard_map/load/pallas_call | solution.py:75
  16.1 2.0 %copy-done = bf16[288,7168]{1,0:T(8,128)(2,1)} copy-done((bf16[288,7168]{1,0:T(8,128)(2,1)}, bf16[288,7168]{1,0:T(8,128)(2,1)S(1)}, u32[]{:S(2)}) %copy-start) | copy-done | bytes 4128792
  18.1 0.1 pad_add_fusion.at_ref
  18.2 2.2 %copy-done.1 = bf16[288,7168]{1,0:T(8,128)(2,1)S(1)} copy-done((bf16[288,7168]{1,0:T(8,128)(2,1)S(1)}, bf16[288,7168]{1,0:T(8,128)(2,1)}, u32[]{:S(2)}) %copy-start.1) | copy-done | bytes 4128792
  20.4 2.9 %shard_map.88.refs_2_ = f32[2,288,128]{2,1,0:T(8,128)S(1)} custom-call(s32[10]{0:T(128)S(1)} %pad_add_fusion.at_ref, bf16[288,7168]{1,0:T(8,128)(2,1)S(1)} %copy-done.1, bf16[288,7168]{1,0:T(8,128)(2,1)} %collective-permute-done.theirs_ref, bf16[896,128]{1,0:T(8,128)(2,1)S(1)} %copy-done.3, bf16[896,128]{1,0:T(8,128)(2,1)S(1)} %collective-permute-done.7.refs_1_), custom_call_target="tpu_custom_call" | custom-call | tf_op jit(solution)/shard_map/pallas_call | solution.py:38
  23.3 0.0 copy-start.4
  23.3 0.0 collective-permute-done.5.refs_0_
  23.3 0.0 collective-permute-done.6.refs_1_
  23.3 2.9 %shard_map.89.part_ref = f32[2,288,128]{2,1,0:T(8,128)S(1)} custom-call(s32[10]{0:T(128)S(1)} %pad_add_fusion.at_ref, bf16[288,7168]{1,0:T(8,128)(2,1)S(1)} %copy-done.1, bf16[288,7168]{1,0:T(8,128)(2,1)} %collective-permute-done.theirs_ref, bf16[896,128]{1,0:T(8,128)(2,1)S(1)} %collective-permute-done.5.refs_0_, ...), custom_call_target="tpu_custom_call" | custom-call | tf_op jit(solution)/shard_map/pallas_call | solution.py:38
  26.3 0.1 collective-permute-start.8
  26.3 0.0 collective-permute-done.3.refs_1_
  26.4 2.9 %shard_map.86.refs_2_ = f32[2,288,128]{2,1,0:T(8,128)S(1)} custom-call(s32[10]{0:T(128)S(1)} %pad_add_fusion.at_ref, bf16[288,7168]{1,0:T(8,128)(2,1)S(1)} %copy-done.1, bf16[288,7168]{1,0:T(8,128)(2,1)} %collective-permute-done.theirs_ref, bf16[896,128]{1,0:T(8,128)(2,1)S(1)} %copy-done.4, bf16[896,128]{1,0:T(8,128)(2,1)S(1)} %collective-permute-done.3.refs_1_), custom_call_target="tpu_custom_call" | custom-call | tf_op jit(solution)/shard_map/pallas_call | solution.py:38
  29.2 0.0 copy-start.7
  29.3 0.0 copy-start.8
  29.3 0.0 copy-start.9
  29.3 0.0 copy-start.6
  29.3 0.0 collective-permute-done.1.refs_0_
  29.3 0.0 collective-permute-done.2.refs_1_
  29.3 3.0 %shard_map.87.part_ref = f32[2,288,128]{2,1,0:T(8,128)S(1)} custom-call(s32[10]{0:T(128)S(1)} %pad_add_fusion.at_ref, bf16[288,7168]{1,0:T(8,128)(2,1)S(1)} %copy-done.1, bf16[288,7168]{1,0:T(8,128)(2,1)} %collective-permute-done.theirs_ref, bf16[896,128]{1,0:T(8,128)(2,1)S(1)} %collective-permute-done.1.refs_0_, ...), custom_call_target="tpu_custom_call" | custom-call | tf_op jit(solution)/shard_map/pallas_call | solution.py:38
  32.4 0.6 collective-permute-start.4
  33.0 0.1 collective-permute-start.9
  33.1 0.0 collective-permute-done.8.other_ref
  33.1 0.2 shard_map.90
  33.3 1.6 %collective-permute-start.10 = (f32[2,128]{1,0:T(2,128)S(1)}, f32[2,128]{1,0:T(2,128)S(1)}, u32[]{:S(2)}, u32[]{:S(2)}) collective-permute-start(f32[2,128]{1,0:T(2,128)S(1)} %get-tuple-element.11.first_ref), channel_id=1, source_target_pairs={{0,1},{1,0},{2,3},{3,2},{4,5},{5,4},{6,7},{7,6},{8,9},{9,8},{10,11... | collective-permute-start | bytes 3080 | tf_op jit(solution)/shard_map/ppermute | solution.py:34
  35.0 2.0 %collective-permute-done.10.second_ref = f32[2,128]{1,0:T(2,128)S(1)} collective-permute-done((f32[2,128]{1,0:T(2,128)S(1)}, f32[2,128]{1,0:T(2,128)S(1)}, u32[]{:S(2)}, u32[]{:S(2)}) %collective-permute-start.10) | collective-permute-done | bytes 1056 | tf_op jit(solution)/shard_map/ppermute | solution.py:34
  37.0 2.6 %collective-permute-start.11 = (f32[4,128]{1,0:T(4,128)S(1)}, f32[4,128]{1,0:T(4,128)S(1)}, u32[]{:S(2)}, u32[]{:S(2)}) collective-permute-start(f32[4,128]{1,0:T(4,128)S(1)} %shard_map.91.refs_0_), channel_id=1, source_target_pairs={{0,2},{1,3},{2,0},{3,1},{4,6},{5,7},{6,4},{7,5},{8,10},{9,11},{10,... | collective-permute-start | bytes 6152 | tf_op jit(solution)/shard_map/ppermute | solution.py:34
  39.5 3.4 %shard_map.93.cols_ref = bf16[4,896,576]{2,1,0:T(8,128)(2,1)S(1)} custom-call(s32[10]{0:T(128)S(1)} %pad_add_fusion.at_ref, bf16[288,7168]{1,0:T(8,128)(2,1)S(1)} %copy-done.2, bf16[288,7168]{1,0:T(8,128)(2,1)} %collective-permute-done.theirs_ref), custom_call_target="tpu_custom_call" | custom-call | tf_op jit(solution)/shard_map/pallas_call | solution.py:38
  43.0 0.0 collective-permute-done.9.other_ref
  43.0 0.0 collective-permute-done.11.refs_1_
  43.0 1.5 %shard_map.92.goal_ref = f32[2,288,128]{2,1,0:T(8,128)S(1)} custom-call(s32[10]{0:T(128)S(1)} %pad_add_fusion.at_ref, f32[2,288,128]{2,1,0:T(8,128)S(1)} %get-tuple-element.10.best_ref, f32[4,288]{1,0:T(4,128)S(1)} %pad_maximum_fusion.scalar_ref, f32[4,288]{1,0:T(4,128)S(1)} %collective-permute-done.9.other_ref, f32[4,128]{1,0:T(4,128)S(1)} %shard_map.91.refs_0_, ...), custom_call_target="tpu_custom_call" | custom-call | tf_op jit(solution)/shard_map/pallas_call | solution.py:38
  44.5 0.0 collective-permute-done.4.other_ref
  44.5 1.0 %shard_map.94 = (bf16[576,128]{1,0:T(8,128)(2,1)S(1)}, f32[288,128]{1,0:T(8,128)S(1)}, bf16[896,128]{1,0:T(8,128)(2,1)S(1)}) custom-call(f32[2,288,128]{2,1,0:T(8,128)S(1)} %shard_map.87.part_ref, f32[2,288,128]{2,1,0:T(8,128)S(1)} %collective-permute-done.4.other_ref, f32[2,288,128]{2,1,0:T(8,128)S(1)} %shard_map.92.goal_ref, ...), custom_call_target="tpu_custom_call" | custom-call | tf_op jit(solution)/shard_map/pallas_call | solution.py:38
  45.5 1.1 %shard_map.95 = (bf16[896,128]{1,0:T(8,128)(2,1)S(1)}, bf16[896,128]{1,0:T(8,128)(2,1)S(1)}, f32[896,128]{1,0:T(8,128)S(1)}) custom-call(bf16[4,896,576]{2,1,0:T(8,128)(2,1)S(1)} %shard_map.93.cols_ref, bf16[576,128]{1,0:T(8,128)(2,1)S(1)} %get-tuple-element.13.grad_ref), custom_call_target="tpu_custom_call" | custom-call | tf_op jit(solution)/shard_map/pallas_call | solution.py:38
  46.5 1.6 %collective-permute-start.13 = (bf16[896,128]{1,0:T(8,128)(2,1)S(1)}, bf16[896,128]{1,0:T(8,128)(2,1)S(1)}, u32[]{:S(2)}, u32[]{:S(2)}) collective-permute-start(bf16[896,128]{1,0:T(8,128)(2,1)S(1)} %get-tuple-element.16), channel_id=1, source_target_pairs={{0,16},{4,20},{8,24},{12,28},{16,0},{20,4},{24,8},{28,12},{1,17},{... | collective-permute-start | bytes 688136 | tf_op jit(solution)/shard_map/ppermute | solution.py:29
  48.1 0.5 collective-permute-start.14
  48.6 1.4 %collective-permute-start.12 = (bf16[896,128]{1,0:T(8,128)(2,1)S(1)}, bf16[896,128]{1,0:T(8,128)(2,1)S(1)}, u32[]{:S(2)}, u32[]{:S(2)}) collective-permute-start(bf16[896,128]{1,0:T(8,128)(2,1)S(1)} %get-tuple-element.15), channel_id=1, source_target_pairs={{0,24},{4,28},{8,16},{12,20},{16,8},{20,12},{24,0},{28,4},{1,25},{... | collective-permute-start | bytes 688136 | tf_op jit(solution)/shard_map/ppermute | solution.py:29
  50.1 4.1 %collective-permute-done.13 = bf16[896,128]{1,0:T(8,128)(2,1)S(1)} collective-permute-done((bf16[896,128]{1,0:T(8,128)(2,1)S(1)}, bf16[896,128]{1,0:T(8,128)(2,1)S(1)}, u32[]{:S(2)}, u32[]{:S(2)}) %collective-permute-start.13) | collective-permute-done | bytes 229408 | tf_op jit(solution)/shard_map/ppermute | solution.py:29
  54.2 2.4 %collective-permute-done.14 = bf16[896,128]{1,0:T(8,128)(2,1)S(1)} collective-permute-done((bf16[896,128]{1,0:T(8,128)(2,1)S(1)}, bf16[896,128]{1,0:T(8,128)(2,1)S(1)}, u32[]{:S(2)}, u32[]{:S(2)}) %collective-permute-start.14) | collective-permute-done | bytes 229408 | tf_op jit(solution)/shard_map/ppermute | solution.py:29
  56.6 2.7 %collective-permute-done.12 = bf16[896,128]{1,0:T(8,128)(2,1)S(1)} collective-permute-done((bf16[896,128]{1,0:T(8,128)(2,1)S(1)}, bf16[896,128]{1,0:T(8,128)(2,1)S(1)}, u32[]{:S(2)}, u32[]{:S(2)}) %collective-permute-start.12) | collective-permute-done | bytes 229408 | tf_op jit(solution)/shard_map/ppermute | solution.py:29
  59.3 0.1 convert_add_fusion
  59.4 0.4 collective-permute-start.15
  59.8 3.6 %collective-permute-start.16 = (bf16[224,128]{1,0:T(8,128)(2,1)S(1)}, bf16[224,128]{1,0:T(8,128)(2,1)S(1)}, u32[]{:S(2)}, u32[]{:S(2)}) collective-permute-start(bf16[224,128]{1,0:T(8,128)(2,1)S(1)} %get-tuple-element.22), channel_id=1, source_target_pairs={{0,3},{1,2},{2,1},{3,0},{4,7},{5,6},{6,5},{7,4},{8,11},{9,10},{10,... | collective-permute-start | bytes 172040 | tf_op jit(solution)/shard_map/ppermute | solution.py:34
  63.4 0.0 collective-permute-start.17
  63.4 1.2 %collective-permute-done.15 = bf16[224,128]{1,0:T(8,128)(2,1)S(1)} collective-permute-done((bf16[224,128]{1,0:T(8,128)(2,1)S(1)}, bf16[224,128]{1,0:T(8,128)(2,1)S(1)}, u32[]{:S(2)}, u32[]{:S(2)}) %collective-permute-start.15) | collective-permute-done | bytes 57376 | tf_op jit(solution)/shard_map/ppermute | solution.py:34
  64.5 1.7 %collective-permute-done.16 = bf16[224,128]{1,0:T(8,128)(2,1)S(1)} collective-permute-done((bf16[224,128]{1,0:T(8,128)(2,1)S(1)}, bf16[224,128]{1,0:T(8,128)(2,1)S(1)}, u32[]{:S(2)}, u32[]{:S(2)}) %collective-permute-start.16) | collective-permute-done | bytes 57376 | tf_op jit(solution)/shard_map/ppermute | solution.py:34
  66.2 1.3 %collective-permute-done.17 = bf16[224,128]{1,0:T(8,128)(2,1)S(1)} collective-permute-done((bf16[224,128]{1,0:T(8,128)(2,1)S(1)}, bf16[224,128]{1,0:T(8,128)(2,1)S(1)}, u32[]{:S(2)}, u32[]{:S(2)}) %collective-permute-start.17) | collective-permute-done | bytes 57376 | tf_op jit(solution)/shard_map/ppermute | solution.py:34
  67.6 0.1 collective-permute-start.18
  67.7 0.7 slice_reduce_fusion
  68.4 3.6 %collective-permute-start.19 = (bf16[224,128]{1,0:T(8,128)(2,1)S(1)}, bf16[224,128]{1,0:T(8,128)(2,1)S(1)}, u32[]{:S(2)}, u32[]{:S(2)}) collective-permute-start(bf16[224,128]{1,0:T(8,128)(2,1)S(1)} %get-tuple-element.19), channel_id=1, source_target_pairs={{0,3},{1,2},{2,1},{3,0},{4,7},{5,6},{6,5},{7,4},{8,11},{9,10},{10,... | collective-permute-start | bytes 172040 | tf_op jit(solution)/shard_map/ppermute | solution.py:34
  72.0 0.0 collective-permute-start.20
  72.0 0.8 collective-permute-done.18
  72.8 1.6 %collective-permute-done.19 = bf16[224,128]{1,0:T(8,128)(2,1)S(1)} collective-permute-done((bf16[224,128]{1,0:T(8,128)(2,1)S(1)}, bf16[224,128]{1,0:T(8,128)(2,1)S(1)}, u32[]{:S(2)}, u32[]{:S(2)}) %collective-permute-start.19) | collective-permute-done | bytes 57376 | tf_op jit(solution)/shard_map/ppermute | solution.py:34
  74.5 1.7 %collective-permute-done.20 = bf16[224,128]{1,0:T(8,128)(2,1)S(1)} collective-permute-done((bf16[224,128]{1,0:T(8,128)(2,1)S(1)}, bf16[224,128]{1,0:T(8,128)(2,1)S(1)}, u32[]{:S(2)}, u32[]{:S(2)}) %collective-permute-start.20) | collective-permute-done | bytes 57376 | tf_op jit(solution)/shard_map/ppermute | solution.py:34
  76.2 0.0 copy-start.5
  76.2 0.8 copy-done.5
  (28 shorter events, 0.2 us)
Async XLA Ops:
  0.6 11.8 %collective-permute-start = (bf16[288,7168]{1,0:T(8,128)(2,1)}, bf16[288,7168]{1,0:T(8,128)(2,1)}, u32[]{:S(2)}, u32[]{:S(2)}) collective-permute-start(bf16[288,7168]{1,0:T(8,128)(2,1)} %features_ref.1), channel_id=1, source_target_pairs={{0,4},{4,0},{8,12},{12,8},{16,20},{20,16},{24,28},{28,24},{1,5},{5... | collective-permute-start | bytes 12386312 | tf_op jit(solution)/shard_map/ppermute | solution.py:29
  1.2 9.2 %collective-permute-start.7 = (bf16[896,128]{1,0:T(8,128)(2,1)}, bf16[896,128]{1,0:T(8,128)(2,1)S(1)}, u32[]{:S(2)}, u32[]{:S(2)}) collective-permute-start(bf16[896,128]{1,0:T(8,128)(2,1)} %refs_0_.3), channel_id=1, source_target_pairs={{0,8},{4,12},{8,0},{12,4},{16,24},{20,28},{24,16},{28,20},{1,9},{5... | collective-permute-start | bytes 688136 | tf_op jit(solution)/shard_map/ppermute | solution.py:29
  3.7 19.5 %collective-permute-start.5 = (bf16[896,128]{1,0:T(8,128)(2,1)}, bf16[896,128]{1,0:T(8,128)(2,1)S(1)}, u32[]{:S(2)}, u32[]{:S(2)}) collective-permute-start(bf16[896,128]{1,0:T(8,128)(2,1)} %refs_0_.3), channel_id=1, source_target_pairs={{0,16},{4,20},{8,24},{12,28},{16,0},{20,4},{24,8},{28,12},{1,17},{... | collective-permute-start | bytes 688136 | tf_op jit(solution)/shard_map/ppermute | solution.py:29
  5.3 18.0 %collective-permute-start.6 = (bf16[896,128]{1,0:T(8,128)(2,1)}, bf16[896,128]{1,0:T(8,128)(2,1)S(1)}, u32[]{:S(2)}, u32[]{:S(2)}) collective-permute-start(bf16[896,128]{1,0:T(8,128)(2,1)} %refs_0_.3), channel_id=1, source_target_pairs={{0,24},{4,28},{8,16},{12,20},{16,8},{20,12},{24,0},{28,4},{1,25},{... | collective-permute-start | bytes 688136 | tf_op jit(solution)/shard_map/ppermute | solution.py:29
  5.3 21.0 %collective-permute-start.3 = (bf16[896,128]{1,0:T(8,128)(2,1)}, bf16[896,128]{1,0:T(8,128)(2,1)S(1)}, u32[]{:S(2)}, u32[]{:S(2)}) collective-permute-start(bf16[896,128]{1,0:T(8,128)(2,1)} %refs_0_.2), channel_id=1, source_target_pairs={{0,8},{4,12},{8,0},{12,4},{16,24},{20,28},{24,16},{28,20},{1,9},{5... | collective-permute-start | bytes 688136 | tf_op jit(solution)/shard_map/ppermute | solution.py:29
  10.4 18.9 %collective-permute-start.1 = (bf16[896,128]{1,0:T(8,128)(2,1)}, bf16[896,128]{1,0:T(8,128)(2,1)S(1)}, u32[]{:S(2)}, u32[]{:S(2)}) collective-permute-start(bf16[896,128]{1,0:T(8,128)(2,1)} %refs_0_.2), channel_id=1, source_target_pairs={{0,16},{4,20},{8,24},{12,28},{16,0},{20,4},{24,8},{28,12},{1,17},{... | collective-permute-start | bytes 688136 | tf_op jit(solution)/shard_map/ppermute | solution.py:29
  12.5 16.9 %collective-permute-start.2 = (bf16[896,128]{1,0:T(8,128)(2,1)}, bf16[896,128]{1,0:T(8,128)(2,1)S(1)}, u32[]{:S(2)}, u32[]{:S(2)}) collective-permute-start(bf16[896,128]{1,0:T(8,128)(2,1)} %refs_0_.2), channel_id=1, source_target_pairs={{0,24},{4,28},{8,16},{12,20},{16,8},{20,12},{24,0},{28,4},{1,25},{... | collective-permute-start | bytes 688136 | tf_op jit(solution)/shard_map/ppermute | solution.py:29
  13.9 4.3 %copy-start.3 = (bf16[896,128]{1,0:T(8,128)(2,1)S(1)}, bf16[896,128]{1,0:T(8,128)(2,1)}, u32[]{:S(2)}) copy-start(bf16[896,128]{1,0:T(8,128)(2,1)} %refs_0_.3) | copy-start | bytes 688132
  16.1 2.0 %copy-start = (bf16[288,7168]{1,0:T(8,128)(2,1)}, bf16[288,7168]{1,0:T(8,128)(2,1)S(1)}, u32[]{:S(2)}) copy-start(bf16[288,7168]{1,0:T(8,128)(2,1)S(1)} %load.1.features_ref) | copy-start | bytes 12386308
  18.2 2.2 %copy-start.1 = (bf16[288,7168]{1,0:T(8,128)(2,1)S(1)}, bf16[288,7168]{1,0:T(8,128)(2,1)}, u32[]{:S(2)}) copy-start(bf16[288,7168]{1,0:T(8,128)(2,1)} %copy-done) | copy-start | bytes 12386308
  23.3 3.1 %copy-start.4 = (bf16[896,128]{1,0:T(8,128)(2,1)S(1)}, bf16[896,128]{1,0:T(8,128)(2,1)}, u32[]{:S(2)}) copy-start(bf16[896,128]{1,0:T(8,128)(2,1)} %refs_0_.2) | copy-start | bytes 688132
  26.3 6.9 %collective-permute-start.8 = (f32[2,288,128]{2,1,0:T(8,128)S(1)}, f32[2,288,128]{2,1,0:T(8,128)S(1)}, u32[]{:S(2)}, u32[]{:S(2)}) collective-permute-start(f32[2,288,128]{2,1,0:T(8,128)S(1)} %shard_map.89.part_ref), channel_id=1, source_target_pairs={{0,4},{4,0},{8,12},{12,8},{16,20},{20,16},{24,28},{28,24},{1,5},{5... | collective-permute-start | bytes 884744 | tf_op jit(solution)/shard_map/ppermute | solution.py:29
  29.2 3.7 %copy-start.7 = (s32[288]{0:T(512)S(1)}, s32[288]{0:T(512)}, u32[]{:S(2)}) copy-start(s32[288]{0:T(512)} %param.10) | copy-start | bytes 3460
  29.3 3.7 %copy-start.8 = (s32[288]{0:T(512)S(1)}, s32[288]{0:T(512)}, u32[]{:S(2)}) copy-start(s32[288]{0:T(512)} %param.11) | copy-start | bytes 3460
  29.3 3.7 %copy-start.9 = (s32[288]{0:T(512)S(1)}, s32[288]{0:T(512)}, u32[]{:S(2)}) copy-start(s32[288]{0:T(512)} %param.13) | copy-start | bytes 3460
  29.3 3.7 %copy-start.6 = (f32[288]{0:T(512)S(1)}, f32[288]{0:T(512)}, u32[]{:S(2)}) copy-start(f32[288]{0:T(512)} %param.12) | copy-start | bytes 3460
  29.3 10.3 %copy-start.2 = (bf16[288,7168]{1,0:T(8,128)(2,1)S(1)}, bf16[288,7168]{1,0:T(8,128)(2,1)}, u32[]{:S(2)}) copy-start(bf16[288,7168]{1,0:T(8,128)(2,1)} %copy-done) | copy-start | bytes 12386308
  32.4 12.1 %collective-permute-start.4 = (f32[2,288,128]{2,1,0:T(8,128)S(1)}, f32[2,288,128]{2,1,0:T(8,128)S(1)}, u32[]{:S(2)}, u32[]{:S(2)}) collective-permute-start(f32[2,288,128]{2,1,0:T(8,128)S(1)} %shard_map.87.part_ref), channel_id=1, source_target_pairs={{0,4},{4,0},{8,12},{12,8},{16,20},{20,16},{24,28},{28,24},{1,5},{5... | collective-permute-start | bytes 884744 | tf_op jit(solution)/shard_map/ppermute | solution.py:29
  33.0 10.0 %collective-permute-start.9 = (f32[4,288]{1,0:T(4,128)S(1)}, f32[4,288]{1,0:T(4,128)S(1)}, u32[]{:S(2)}, u32[]{:S(2)}) collective-permute-start(f32[4,288]{1,0:T(4,128)S(1)} %pad_maximum_fusion.scalar_ref), channel_id=1, source_target_pairs={{0,4},{4,0},{8,12},{12,8},{16,20},{20,16},{24,28},{28,24},{1,5},{5... | collective-permute-start | bytes 13832 | tf_op jit(solution)/shard_map/ppermute | solution.py:29
  33.3 3.6 %collective-permute-start.10 = (f32[2,128]{1,0:T(2,128)S(1)}, f32[2,128]{1,0:T(2,128)S(1)}, u32[]{:S(2)}, u32[]{:S(2)}) collective-permute-start(f32[2,128]{1,0:T(2,128)S(1)} %get-tuple-element.11.first_ref), channel_id=1, source_target_pairs={{0,1},{1,0},{2,3},{3,2},{4,5},{5,4},{6,7},{7,6},{8,9},{9,8},{10,11... | collective-permute-start | bytes 3080 | tf_op jit(solution)/shard_map/ppermute | solution.py:34
  37.0 6.1 %collective-permute-start.11 = (f32[4,128]{1,0:T(4,128)S(1)}, f32[4,128]{1,0:T(4,128)S(1)}, u32[]{:S(2)}, u32[]{:S(2)}) collective-permute-start(f32[4,128]{1,0:T(4,128)S(1)} %shard_map.91.refs_0_), channel_id=1, source_target_pairs={{0,2},{1,3},{2,0},{3,1},{4,6},{5,7},{6,4},{7,5},{8,10},{9,11},{10,... | collective-permute-start | bytes 6152 | tf_op jit(solution)/shard_map/ppermute | solution.py:34
  46.5 7.6 %collective-permute-start.13 = (bf16[896,128]{1,0:T(8,128)(2,1)S(1)}, bf16[896,128]{1,0:T(8,128)(2,1)S(1)}, u32[]{:S(2)}, u32[]{:S(2)}) collective-permute-start(bf16[896,128]{1,0:T(8,128)(2,1)S(1)} %get-tuple-element.16), channel_id=1, source_target_pairs={{0,16},{4,20},{8,24},{12,28},{16,0},{20,4},{24,8},{28,12},{1,17},{... | collective-permute-start | bytes 688136 | tf_op jit(solution)/shard_map/ppermute | solution.py:29
  48.1 8.5 %collective-permute-start.14 = (bf16[896,128]{1,0:T(8,128)(2,1)S(1)}, bf16[896,128]{1,0:T(8,128)(2,1)S(1)}, u32[]{:S(2)}, u32[]{:S(2)}) collective-permute-start(bf16[896,128]{1,0:T(8,128)(2,1)S(1)} %get-tuple-element.17), channel_id=1, source_target_pairs={{0,8},{4,12},{8,0},{12,4},{16,24},{20,28},{24,16},{28,20},{1,9},{5... | collective-permute-start | bytes 688136 | tf_op jit(solution)/shard_map/ppermute | solution.py:29
  48.6 10.6 %collective-permute-start.12 = (bf16[896,128]{1,0:T(8,128)(2,1)S(1)}, bf16[896,128]{1,0:T(8,128)(2,1)S(1)}, u32[]{:S(2)}, u32[]{:S(2)}) collective-permute-start(bf16[896,128]{1,0:T(8,128)(2,1)S(1)} %get-tuple-element.15), channel_id=1, source_target_pairs={{0,24},{4,28},{8,16},{12,20},{16,8},{20,12},{24,0},{28,4},{1,25},{... | collective-permute-start | bytes 688136 | tf_op jit(solution)/shard_map/ppermute | solution.py:29
  59.4 5.2 %collective-permute-start.15 = (bf16[224,128]{1,0:T(8,128)(2,1)S(1)}, bf16[224,128]{1,0:T(8,128)(2,1)S(1)}, u32[]{:S(2)}, u32[]{:S(2)}) collective-permute-start(bf16[224,128]{1,0:T(8,128)(2,1)S(1)} %get-tuple-element.20), channel_id=1, source_target_pairs={{0,2},{1,3},{2,0},{3,1},{4,6},{5,7},{6,4},{7,5},{8,10},{9,11},{10,... | collective-permute-start | bytes 172040 | tf_op jit(solution)/shard_map/ppermute | solution.py:34
  59.8 6.5 %collective-permute-start.16 = (bf16[224,128]{1,0:T(8,128)(2,1)S(1)}, bf16[224,128]{1,0:T(8,128)(2,1)S(1)}, u32[]{:S(2)}, u32[]{:S(2)}) collective-permute-start(bf16[224,128]{1,0:T(8,128)(2,1)S(1)} %get-tuple-element.22), channel_id=1, source_target_pairs={{0,3},{1,2},{2,1},{3,0},{4,7},{5,6},{6,5},{7,4},{8,11},{9,10},{10,... | collective-permute-start | bytes 172040 | tf_op jit(solution)/shard_map/ppermute | solution.py:34
  63.4 4.2 %collective-permute-start.17 = (bf16[224,128]{1,0:T(8,128)(2,1)S(1)}, bf16[224,128]{1,0:T(8,128)(2,1)S(1)}, u32[]{:S(2)}, u32[]{:S(2)}) collective-permute-start(bf16[224,128]{1,0:T(8,128)(2,1)S(1)} %get-tuple-element.21), channel_id=1, source_target_pairs={{0,1},{1,0},{2,3},{3,2},{4,5},{5,4},{6,7},{7,6},{8,9},{9,8},{10,11... | collective-permute-start | bytes 172040 | tf_op jit(solution)/shard_map/ppermute | solution.py:34
  67.6 5.1 %collective-permute-start.18 = (bf16[224,128]{1,0:T(8,128)(2,1)S(1)}, bf16[224,128]{1,0:T(8,128)(2,1)S(1)}, u32[]{:S(2)}, u32[]{:S(2)}) collective-permute-start(bf16[224,128]{1,0:T(8,128)(2,1)S(1)} %get-tuple-element.19), channel_id=1, source_target_pairs={{0,2},{1,3},{2,0},{3,1},{4,6},{5,7},{6,4},{7,5},{8,10},{9,11},{10,... | collective-permute-start | bytes 172040 | tf_op jit(solution)/shard_map/ppermute | solution.py:34
  68.4 6.0 %collective-permute-start.19 = (bf16[224,128]{1,0:T(8,128)(2,1)S(1)}, bf16[224,128]{1,0:T(8,128)(2,1)S(1)}, u32[]{:S(2)}, u32[]{:S(2)}) collective-permute-start(bf16[224,128]{1,0:T(8,128)(2,1)S(1)} %get-tuple-element.19), channel_id=1, source_target_pairs={{0,3},{1,2},{2,1},{3,0},{4,7},{5,6},{6,5},{7,4},{8,11},{9,10},{10,... | collective-permute-start | bytes 172040 | tf_op jit(solution)/shard_map/ppermute | solution.py:34
  72.0 4.2 %collective-permute-start.20 = (bf16[224,128]{1,0:T(8,128)(2,1)S(1)}, bf16[224,128]{1,0:T(8,128)(2,1)S(1)}, u32[]{:S(2)}, u32[]{:S(2)}) collective-permute-start(bf16[224,128]{1,0:T(8,128)(2,1)S(1)} %get-tuple-element.19), channel_id=1, source_target_pairs={{0,1},{1,0},{2,3},{3,2},{4,5},{5,4},{6,7},{7,6},{8,9},{9,8},{10,11... | collective-permute-start | bytes 172040 | tf_op jit(solution)/shard_map/ppermute | solution.py:34
  76.2 0.8 %copy-start.5 = (f32[896,128]{1,0:T(8,128)}, f32[896,128]{1,0:T(8,128)S(1)}, u32[]{:S(2)}) copy-start(f32[896,128]{1,0:T(8,128)S(1)} %convert_dynamic-update-slice_fusion) | copy-start | bytes 1376260

commit v3 on v2

--- a/solution.py
+++ b/solution.py
@@ -53,42 +53,43 @@
     return pltpu.VMEM(dims, dtype)
 
 
-def relay_order(chips):
-    return sorted(range(1, chips), key=lambda o: (bin(o).count("1"), o))
-
-
 def direct_hops(shard, chips):
-    return {0: (shard,), **{o: (across(shard, 2 * o),) for o in relay_order(chips)}}
+    held = {0: (shard,)}
+    for offset in range(1, chips):
+        held[offset] = (across(shard, 2 * offset),)
+    return held
 
 
 def column(ref, at_ref, offset, width):
     return ref.at[:, pl.ds(pl.multiple_of(at_ref[offset] * width, width), width)]
 
 
-def load_kernel(features_ref, out_ref, sem):
-    copy = pltpu.make_async_copy(features_ref, out_ref, sem)
-    copy.start()
-    copy.wait()
-
-
-def loaded(features):
+def turn_kernel(at_ref, features_ref, theirs_ref, kept_ref, out_ref, sems):
+    chips, width, _ = out_ref.shape
+    columns = [(column(features_ref, at_ref, j, width), column(kept_ref, at_ref, j, width)) for j in range(chips)]
+    copies = [pltpu.make_async_copy(*pair, sems.at[j]) for j, pair in enumerate(columns)]
+    for copy in copies:
+        copy.start()
+    for j, copy in enumerate(copies):
+        copy.wait()
+        both = [column(ref, at_ref, j, width)[...] for ref in (kept_ref, theirs_ref)]
+        out_ref[j] = jnp.concatenate(both, axis=0).T
+
+
+def turned(at, features, theirs, chips, width):
+    rows = features.shape[0]
     return pl.pallas_call(
-        load_kernel,
-        out_shape=shape(*features.shape, dtype=features.dtype),
-        in_specs=[ANY],
-        out_specs=VMEM,
-        scratch_shapes=[pltpu.SemaphoreType.DMA],
+        turn_kernel,
+        out_shape=(
+            shape(*features.shape, dtype=features.dtype),
+            shape(chips, width, 2 * rows, dtype=features.dtype),
+        ),
+        in_specs=[SMEM, ANY, VMEM],
+        out_specs=(VMEM, VMEM),
+        scratch_shapes=[pltpu.SemaphoreType.DMA((chips,))],
         compiler_params=pltpu.CompilerParams(vmem_limit_bytes=16 * MIB),
-        name="load",
-    )(pltpu.with_memory_space_constraint(features, pltpu.HBM))
-
-
-def turn_kernel(at_ref, features_ref, theirs_ref, out_ref):
-    chips, width, _ = out_ref.shape
-    for j in range(chips):
-        both = [column(ref, at_ref, j, width)[...] for ref in (features_ref, theirs_ref)]
-        both = jnp.concatenate(both, axis=0)
-        out_ref[j] = both.T
+        name="turn_columns",
+    )(at, pltpu.with_memory_space_constraint(features, pltpu.HBM), kept(theirs))
 
 
 def logits_kernel(width, offsets, has_start, at_ref, features_ref, theirs_ref, *refs):
@@ -273,9 +274,7 @@
         ]
     )
     scalars = (scalars, across(scalars, 1))
-    features = loaded(features)
-    out = shape(chips, head_rows, 2 * tokens, dtype=features.dtype)
-    cols_turned = call(turn_kernel, out, at, features, theirs, smem=1)
+    features, cols_turned = turned(at, features, theirs, chips, head_rows)
 
     last = chips - 1
     both = shape(2, tokens, bins)

time: 77.2 us -> 74.2 us (0.961)
  local copies, waits for them, and re-layouts: 5.78 us -> 1.6 us
  waiting for transfers between devices: 22.7 us -> 24.8 us
  Pallas kernels: 21.1 us -> 20 us
    unnamed x20 -> x14, local copies, waits for them, and re-layouts: 4.97 us -> 0.8 us
    pallas_call x10 -> x9, Pallas kernels: 18.8 us -> 15.3 us  [call(): pl.pallas_call(kernel, out_shape=outs, scratch_shapes=scratch, in_specs=[...]
    ppermute x8, waiting for transfers between devices: 10.3 us -> 13.3 us  [mixed(): return lax.ppermute(value, 'mp', [(i, i ^ mask) for i in range(count)])]
    pallas_call x1, Pallas kernels: 2.22 us -> 4.76 us  [turned(): pl.pallas_call(turn_kernel, out_shape=(shape(*features.shape, dtype=featu...]
    ppermute x13, waiting for transfers between devices: 12.4 us -> 11.5 us  [across(): return lax.ppermute(value, 'dp', [(i, i ^ mask) for i in range(count)])]
  transfers between devices with their start and end apart: 21 -> 21, of which waited for: 11 -> 12; matrix products, arithmetic and copies ran while one was open for 1% -> 1% of each run, Pallas kernels for 25% -> 24%
where the time goes in v3:
time: 74.2 us; the launch traced here: 74 us
  starting transfers between devices  26.4 us (36%)
  waiting for transfers between devices  24.8 us (33%)
  Pallas kernels  20 us (27%)
  local copies, waits for them, and re-layouts  1.6 us (2%)
  between operations  0.91 us (1%)
    pallas_call x9, Pallas kernels, call(): pl.pallas_call(kernel, out_shape=outs, scratch_shapes=scratch, in_specs=[...  15.3 us
    ppermute x13, starting transfers between devices, across(): return lax.ppermute(value, 'dp', [(i, i ^ mask) for i in range(count)])  14.4 us
    ppermute x8, waiting for transfers between devices, mixed(): return lax.ppermute(value, 'mp', [(i, i ^ mask) for i in range(count)])  13.3 us
    ppermute x8, starting transfers between devices, mixed(): return lax.ppermute(value, 'mp', [(i, i ^ mask) for i in range(count)])  12 us
    ppermute x13, waiting for transfers between devices, across(): return lax.ppermute(value, 'dp', [(i, i ^ mask) for i in range(count)])  11.5 us
    pallas_call x1, Pallas kernels, turned(): pl.pallas_call(turn_kernel, out_shape=(shape(*features.shape, dtype=featu...  4.76 us
  transfers between devices with their start and end apart: 21, of which 12 were waited for; matrix products, arithmetic and copies ran while one was open for 1% of the time, Pallas kernels for 24%

profile of v3, /device:TPU:0, one launch (start us, length us, event | category | flops | bytes accessed | tf_op | source)
XLA Modules:
  0.0 74.0 jit_solution(14093043265698470770)
XLA Ops:
  0.6 0.6 collective-permute-start
  1.2 2.6 %collective-permute-start.7 = (bf16[896,128]{1,0:T(8,128)(2,1)}, bf16[896,128]{1,0:T(8,128)(2,1)S(1)}, u32[]{:S(2)}, u32[]{:S(2)}) collective-permute-start(bf16[896,128]{1,0:T(8,128)(2,1)} %refs_0_.3), channel_id=1, source_target_pairs={{0,8},{4,12},{8,0},{12,4},{16,24},{20,28},{24,16},{28,20},{1,9},{5... | collective-permute-start | bytes 688136 | tf_op jit(solution)/shard_map/ppermute | solution.py:29
  3.7 1.5 %collective-permute-start.5 = (bf16[896,128]{1,0:T(8,128)(2,1)}, bf16[896,128]{1,0:T(8,128)(2,1)S(1)}, u32[]{:S(2)}, u32[]{:S(2)}) collective-permute-start(bf16[896,128]{1,0:T(8,128)(2,1)} %refs_0_.3), channel_id=1, source_target_pairs={{0,16},{4,20},{8,24},{12,28},{16,0},{20,4},{24,8},{28,12},{1,17},{... | collective-permute-start | bytes 688136 | tf_op jit(solution)/shard_map/ppermute | solution.py:29
  5.3 0.0 collective-permute-start.6
  5.3 1.9 %collective-permute-start.3 = (bf16[896,128]{1,0:T(8,128)(2,1)}, bf16[896,128]{1,0:T(8,128)(2,1)S(1)}, u32[]{:S(2)}, u32[]{:S(2)}) collective-permute-start(bf16[896,128]{1,0:T(8,128)(2,1)} %refs_0_.2), channel_id=1, source_target_pairs={{0,8},{4,12},{8,0},{12,4},{16,24},{20,28},{24,16},{28,20},{1,9},{5... | collective-permute-start | bytes 688136 | tf_op jit(solution)/shard_map/ppermute | solution.py:29
  7.2 3.2 %collective-permute-done.7.refs_1_ = bf16[896,128]{1,0:T(8,128)(2,1)S(1)} collective-permute-done((bf16[896,128]{1,0:T(8,128)(2,1)}, bf16[896,128]{1,0:T(8,128)(2,1)S(1)}, u32[]{:S(2)}, u32[]{:S(2)}) %collective-permute-start.7) | collective-permute-done | bytes 229408 | tf_op jit(solution)/shard_map/ppermute | solution.py:29
  10.4 2.0 %collective-permute-start.1 = (bf16[896,128]{1,0:T(8,128)(2,1)}, bf16[896,128]{1,0:T(8,128)(2,1)S(1)}, u32[]{:S(2)}, u32[]{:S(2)}) collective-permute-start(bf16[896,128]{1,0:T(8,128)(2,1)} %refs_0_.2), channel_id=1, source_target_pairs={{0,16},{4,20},{8,24},{12,28},{16,0},{20,4},{24,8},{28,12},{1,17},{... | collective-permute-start | bytes 688136 | tf_op jit(solution)/shard_map/ppermute | solution.py:29
  12.5 0.0 collective-permute-done.theirs_ref
  12.5 1.4 %collective-permute-start.2 = (bf16[896,128]{1,0:T(8,128)(2,1)}, bf16[896,128]{1,0:T(8,128)(2,1)S(1)}, u32[]{:S(2)}, u32[]{:S(2)}) collective-permute-start(bf16[896,128]{1,0:T(8,128)(2,1)} %refs_0_.2), channel_id=1, source_target_pairs={{0,24},{4,28},{8,16},{12,20},{16,8},{20,12},{24,0},{28,4},{1,25},{... | collective-permute-start | bytes 688136 | tf_op jit(solution)/shard_map/ppermute | solution.py:29
  13.9 0.1 pad_add_fusion.at_ref
  14.0 4.8 %turn_columns.1 = (bf16[288,7168]{1,0:T(8,128)(2,1)S(1)}, bf16[4,896,576]{2,1,0:T(8,128)(2,1)S(1)}) custom-call(s32[10]{0:T(128)S(1)} %pad_add_fusion.at_ref, bf16[288,7168]{1,0:T(8,128)(2,1)} %features_ref.1, bf16[288,7168]{1,0:T(8,128)(2,1)} %collective-permute-done.theirs_ref), custom_call_target="tpu_custom_call" | custom-call | tf_op jit(solution)/shard_map/turn_columns/pallas_call | solution.py:81
  18.8 0.0 copy-done
  18.8 2.9 %shard_map.88.refs_2_ = f32[2,288,128]{2,1,0:T(8,128)S(1)} custom-call(s32[10]{0:T(128)S(1)} %pad_add_fusion.at_ref, bf16[288,7168]{1,0:T(8,128)(2,1)S(1)} %get-tuple-element.12.features_ref, bf16[288,7168]{1,0:T(8,128)(2,1)} %collective-permute-done.theirs_ref, bf16[896,128]{1,0:T(8,128)(2,1)S(1)} %copy-done, ...), custom_call_target="tpu_custom_call" | custom-call | tf_op jit(solution)/shard_map/pallas_call | solution.py:38
  21.7 0.0 copy-start.1
  21.7 0.0 collective-permute-done.5.refs_0_
  21.7 0.0 collective-permute-done.6.refs_1_
  21.7 2.9 %shard_map.89.part_ref = f32[2,288,128]{2,1,0:T(8,128)S(1)} custom-call(s32[10]{0:T(128)S(1)} %pad_add_fusion.at_ref, bf16[288,7168]{1,0:T(8,128)(2,1)S(1)} %get-tuple-element.12.features_ref, bf16[288,7168]{1,0:T(8,128)(2,1)} %collective-permute-done.theirs_ref, bf16[896,128]{1,0:T(8,128)(2,1)S(1)} %collective-permute-done.5.refs_0_, ...), custom_call_target="tpu_custom_call" | custom-call | tf_op jit(solution)/shard_map/pallas_call | solution.py:38
  24.6 0.1 collective-permute-start.8
  24.7 0.0 collective-permute-done.3.refs_1_
  24.7 0.0 copy-done.1
  24.7 2.9 %shard_map.86.refs_2_ = f32[2,288,128]{2,1,0:T(8,128)S(1)} custom-call(s32[10]{0:T(128)S(1)} %pad_add_fusion.at_ref, bf16[288,7168]{1,0:T(8,128)(2,1)S(1)} %get-tuple-element.12.features_ref, bf16[288,7168]{1,0:T(8,128)(2,1)} %collective-permute-done.theirs_ref, bf16[896,128]{1,0:T(8,128)(2,1)S(1)} %copy-done.1, ...), custom_call_target="tpu_custom_call" | custom-call | tf_op jit(solution)/shard_map/pallas_call | solution.py:38
  27.6 0.0 copy-start.4
  27.6 0.0 copy-start.5
  27.6 0.0 copy-start.6
  27.7 0.0 copy-start.3
  27.7 0.0 collective-permute-done.1.refs_0_
  27.7 0.0 collective-permute-done.2.refs_1_
  27.7 2.9 %shard_map.87.part_ref = f32[2,288,128]{2,1,0:T(8,128)S(1)} custom-call(s32[10]{0:T(128)S(1)} %pad_add_fusion.at_ref, bf16[288,7168]{1,0:T(8,128)(2,1)S(1)} %get-tuple-element.12.features_ref, bf16[288,7168]{1,0:T(8,128)(2,1)} %collective-permute-done.theirs_ref, bf16[896,128]{1,0:T(8,128)(2,1)S(1)} %collective-permute-done.1.refs_0_, ...), custom_call_target="tpu_custom_call" | custom-call | tf_op jit(solution)/shard_map/pallas_call | solution.py:38
  30.6 0.6 collective-permute-start.4
  31.2 0.0 copy-done.3
  31.3 0.1 collective-permute-start.9
  31.4 0.0 collective-permute-done.8.other_ref
  31.4 0.2 shard_map.90
  31.5 1.6 %collective-permute-start.10 = (f32[2,128]{1,0:T(2,128)S(1)}, f32[2,128]{1,0:T(2,128)S(1)}, u32[]{:S(2)}, u32[]{:S(2)}) collective-permute-start(f32[2,128]{1,0:T(2,128)S(1)} %get-tuple-element.14.first_ref), channel_id=1, source_target_pairs={{0,1},{1,0},{2,3},{3,2},{4,5},{5,4},{6,7},{7,6},{8,9},{9,8},{10,11... | collective-permute-start | bytes 3080 | tf_op jit(solution)/shard_map/ppermute | solution.py:34
  33.2 2.0 %collective-permute-done.10.second_ref = f32[2,128]{1,0:T(2,128)S(1)} collective-permute-done((f32[2,128]{1,0:T(2,128)S(1)}, f32[2,128]{1,0:T(2,128)S(1)}, u32[]{:S(2)}, u32[]{:S(2)}) %collective-permute-start.10) | collective-permute-done | bytes 1056 | tf_op jit(solution)/shard_map/ppermute | solution.py:34
  35.2 2.6 %collective-permute-start.11 = (f32[4,128]{1,0:T(4,128)S(1)}, f32[4,128]{1,0:T(4,128)S(1)}, u32[]{:S(2)}, u32[]{:S(2)}) collective-permute-start(f32[4,128]{1,0:T(4,128)S(1)} %shard_map.91.refs_0_), channel_id=1, source_target_pairs={{0,2},{1,3},{2,0},{3,1},{4,6},{5,7},{6,4},{7,5},{8,10},{9,11},{10,... | collective-permute-start | bytes 6152 | tf_op jit(solution)/shard_map/ppermute | solution.py:34
  37.8 0.0 collective-permute-done.9.other_ref
  37.8 1.9 %collective-permute-done.11.refs_1_ = f32[4,128]{1,0:T(4,128)S(1)} collective-permute-done((f32[4,128]{1,0:T(4,128)S(1)}, f32[4,128]{1,0:T(4,128)S(1)}, u32[]{:S(2)}, u32[]{:S(2)}) %collective-permute-start.11) | collective-permute-done | bytes 2080 | tf_op jit(solution)/shard_map/ppermute | solution.py:34
  39.7 1.5 %shard_map.92.goal_ref = f32[2,288,128]{2,1,0:T(8,128)S(1)} custom-call(s32[10]{0:T(128)S(1)} %pad_add_fusion.at_ref, f32[2,288,128]{2,1,0:T(8,128)S(1)} %get-tuple-element.13.best_ref, f32[4,288]{1,0:T(4,128)S(1)} %pad_maximum_fusion.scalar_ref, f32[4,288]{1,0:T(4,128)S(1)} %collective-permute-done.9.other_ref, f32[4,128]{1,0:T(4,128)S(1)} %shard_map.91.refs_0_, ...), custom_call_target="tpu_custom_call" | custom-call | tf_op jit(solution)/shard_map/pallas_call | solution.py:38
  41.1 0.0 collective-permute-done.4.other_ref
  41.1 1.0 %shard_map.93 = (bf16[576,128]{1,0:T(8,128)(2,1)S(1)}, f32[288,128]{1,0:T(8,128)S(1)}, bf16[896,128]{1,0:T(8,128)(2,1)S(1)}) custom-call(f32[2,288,128]{2,1,0:T(8,128)S(1)} %shard_map.87.part_ref, f32[2,288,128]{2,1,0:T(8,128)S(1)} %collective-permute-done.4.other_ref, f32[2,288,128]{2,1,0:T(8,128)S(1)} %shard_map.92.goal_ref, ...), custom_call_target="tpu_custom_call" | custom-call | tf_op jit(solution)/shard_map/pallas_call | solution.py:38
  42.1 1.1 %shard_map.94 = (bf16[896,128]{1,0:T(8,128)(2,1)S(1)}, bf16[896,128]{1,0:T(8,128)(2,1)S(1)}, f32[896,128]{1,0:T(8,128)S(1)}) custom-call(bf16[4,896,576]{2,1,0:T(8,128)(2,1)S(1)} %get-tuple-element.15.cols_ref, bf16[576,128]{1,0:T(8,128)(2,1)S(1)} %get-tuple-element.17.grad_ref), custom_call_target="tpu_custom_call" | custom-call | tf_op jit(solution)/shard_map/pallas_call | solution.py:38
  43.2 1.6 %collective-permute-start.13 = (bf16[896,128]{1,0:T(8,128)(2,1)S(1)}, bf16[896,128]{1,0:T(8,128)(2,1)S(1)}, u32[]{:S(2)}, u32[]{:S(2)}) collective-permute-start(bf16[896,128]{1,0:T(8,128)(2,1)S(1)} %get-tuple-element.20), channel_id=1, source_target_pairs={{0,16},{4,20},{8,24},{12,28},{16,0},{20,4},{24,8},{28,12},{1,17},{... | collective-permute-start | bytes 688136 | tf_op jit(solution)/shard_map/ppermute | solution.py:29
  44.7 0.6 collective-permute-start.14
  45.3 1.4 %collective-permute-start.12 = (bf16[896,128]{1,0:T(8,128)(2,1)S(1)}, bf16[896,128]{1,0:T(8,128)(2,1)S(1)}, u32[]{:S(2)}, u32[]{:S(2)}) collective-permute-start(bf16[896,128]{1,0:T(8,128)(2,1)S(1)} %get-tuple-element.19), channel_id=1, source_target_pairs={{0,24},{4,28},{8,16},{12,20},{16,8},{20,12},{24,0},{28,4},{1,25},{... | collective-permute-start | bytes 688136 | tf_op jit(solution)/shard_map/ppermute | solution.py:29
  46.7 4.8 %collective-permute-done.13 = bf16[896,128]{1,0:T(8,128)(2,1)S(1)} collective-permute-done((bf16[896,128]{1,0:T(8,128)(2,1)S(1)}, bf16[896,128]{1,0:T(8,128)(2,1)S(1)}, u32[]{:S(2)}, u32[]{:S(2)}) %collective-permute-start.13) | collective-permute-done | bytes 229408 | tf_op jit(solution)/shard_map/ppermute | solution.py:29
  51.5 1.1 %collective-permute-done.14 = bf16[896,128]{1,0:T(8,128)(2,1)S(1)} collective-permute-done((bf16[896,128]{1,0:T(8,128)(2,1)S(1)}, bf16[896,128]{1,0:T(8,128)(2,1)S(1)}, u32[]{:S(2)}, u32[]{:S(2)}) %collective-permute-start.14) | collective-permute-done | bytes 229408 | tf_op jit(solution)/shard_map/ppermute | solution.py:29
  52.6 2.4 %collective-permute-done.12 = bf16[896,128]{1,0:T(8,128)(2,1)S(1)} collective-permute-done((bf16[896,128]{1,0:T(8,128)(2,1)S(1)}, bf16[896,128]{1,0:T(8,128)(2,1)S(1)}, u32[]{:S(2)}, u32[]{:S(2)}) %collective-permute-start.12) | collective-permute-done | bytes 229408 | tf_op jit(solution)/shard_map/ppermute | solution.py:29
  55.0 0.1 convert_add_fusion
  55.2 2.6 %collective-permute-start.15 = (bf16[224,128]{1,0:T(8,128)(2,1)S(1)}, bf16[224,128]{1,0:T(8,128)(2,1)S(1)}, u32[]{:S(2)}, u32[]{:S(2)}) collective-permute-start(bf16[224,128]{1,0:T(8,128)(2,1)S(1)} %get-tuple-element.24), channel_id=1, source_target_pairs={{0,2},{1,3},{2,0},{3,1},{4,6},{5,7},{6,4},{7,5},{8,10},{9,11},{10,... | collective-permute-start | bytes 172040 | tf_op jit(solution)/shard_map/ppermute | solution.py:34
  57.8 1.4 %collective-permute-start.16 = (bf16[224,128]{1,0:T(8,128)(2,1)S(1)}, bf16[224,128]{1,0:T(8,128)(2,1)S(1)}, u32[]{:S(2)}, u32[]{:S(2)}) collective-permute-start(bf16[224,128]{1,0:T(8,128)(2,1)S(1)} %get-tuple-element.26), channel_id=1, source_target_pairs={{0,3},{1,2},{2,1},{3,0},{4,7},{5,6},{6,5},{7,4},{8,11},{9,10},{10,... | collective-permute-start | bytes 172040 | tf_op jit(solution)/shard_map/ppermute | solution.py:34
  59.2 0.2 collective-permute-start.17
  59.4 0.9 %collective-permute-done.15 = bf16[224,128]{1,0:T(8,128)(2,1)S(1)} collective-permute-done((bf16[224,128]{1,0:T(8,128)(2,1)S(1)}, bf16[224,128]{1,0:T(8,128)(2,1)S(1)}, u32[]{:S(2)}, u32[]{:S(2)}) %collective-permute-start.15) | collective-permute-done | bytes 57376 | tf_op jit(solution)/shard_map/ppermute | solution.py:34
  60.3 3.6 %collective-permute-done.16 = bf16[224,128]{1,0:T(8,128)(2,1)S(1)} collective-permute-done((bf16[224,128]{1,0:T(8,128)(2,1)S(1)}, bf16[224,128]{1,0:T(8,128)(2,1)S(1)}, u32[]{:S(2)}, u32[]{:S(2)}) %collective-permute-start.16) | collective-permute-done | bytes 57376 | tf_op jit(solution)/shard_map/ppermute | solution.py:34
  63.9 0.4 collective-permute-done.17
  64.4 1.5 %collective-permute-start.18 = (bf16[224,128]{1,0:T(8,128)(2,1)S(1)}, bf16[224,128]{1,0:T(8,128)(2,1)S(1)}, u32[]{:S(2)}, u32[]{:S(2)}) collective-permute-start(bf16[224,128]{1,0:T(8,128)(2,1)S(1)} %get-tuple-element.23), channel_id=1, source_target_pairs={{0,2},{1,3},{2,0},{3,1},{4,6},{5,7},{6,4},{7,5},{8,10},{9,11},{10,... | collective-permute-start | bytes 172040 | tf_op jit(solution)/shard_map/ppermute | solution.py:34
  65.9 0.7 slice_reduce_fusion
  66.6 2.0 %collective-permute-start.19 = (bf16[224,128]{1,0:T(8,128)(2,1)S(1)}, bf16[224,128]{1,0:T(8,128)(2,1)S(1)}, u32[]{:S(2)}, u32[]{:S(2)}) collective-permute-start(bf16[224,128]{1,0:T(8,128)(2,1)S(1)} %get-tuple-element.23), channel_id=1, source_target_pairs={{0,3},{1,2},{2,1},{3,0},{4,7},{5,6},{6,5},{7,4},{8,11},{9,10},{10,... | collective-permute-start | bytes 172040 | tf_op jit(solution)/shard_map/ppermute | solution.py:34
  68.6 0.1 collective-permute-start.20
  68.7 1.5 %collective-permute-done.18 = bf16[224,128]{1,0:T(8,128)(2,1)S(1)} collective-permute-done((bf16[224,128]{1,0:T(8,128)(2,1)S(1)}, bf16[224,128]{1,0:T(8,128)(2,1)S(1)}, u32[]{:S(2)}, u32[]{:S(2)}) %collective-permute-start.18) | collective-permute-done | bytes 57376 | tf_op jit(solution)/shard_map/ppermute | solution.py:34
  70.1 2.5 %collective-permute-done.19 = bf16[224,128]{1,0:T(8,128)(2,1)S(1)} collective-permute-done((bf16[224,128]{1,0:T(8,128)(2,1)S(1)}, bf16[224,128]{1,0:T(8,128)(2,1)S(1)}, u32[]{:S(2)}, u32[]{:S(2)}) %collective-permute-start.19) | collective-permute-done | bytes 57376 | tf_op jit(solution)/shard_map/ppermute | solution.py:34
  72.6 0.6 collective-permute-done.20
  73.2 0.0 copy-start.2
  73.2 0.8 %copy-done.2 = f32[896,128]{1,0:T(8,128)} copy-done((f32[896,128]{1,0:T(8,128)}, f32[896,128]{1,0:T(8,128)S(1)}, u32[]{:S(2)}) %copy-start.2) | copy-done | bytes 458776
  (21 shorter events, 0.2 us)
Async XLA Ops:
  0.6 11.8 %collective-permute-start = (bf16[288,7168]{1,0:T(8,128)(2,1)}, bf16[288,7168]{1,0:T(8,128)(2,1)}, u32[]{:S(2)}, u32[]{:S(2)}) collective-permute-start(bf16[288,7168]{1,0:T(8,128)(2,1)} %features_ref.1), channel_id=1, source_target_pairs={{0,4},{4,0},{8,12},{12,8},{16,20},{20,16},{24,28},{28,24},{1,5},{5... | collective-permute-start | bytes 12386312 | tf_op jit(solution)/shard_map/ppermute | solution.py:29
  1.2 9.2 %collective-permute-start.7 = (bf16[896,128]{1,0:T(8,128)(2,1)}, bf16[896,128]{1,0:T(8,128)(2,1)S(1)}, u32[]{:S(2)}, u32[]{:S(2)}) collective-permute-start(bf16[896,128]{1,0:T(8,128)(2,1)} %refs_0_.3), channel_id=1, source_target_pairs={{0,8},{4,12},{8,0},{12,4},{16,24},{20,28},{24,16},{28,20},{1,9},{5... | collective-permute-start | bytes 688136 | tf_op jit(solution)/shard_map/ppermute | solution.py:29
  3.7 17.9 %collective-permute-start.5 = (bf16[896,128]{1,0:T(8,128)(2,1)}, bf16[896,128]{1,0:T(8,128)(2,1)S(1)}, u32[]{:S(2)}, u32[]{:S(2)}) collective-permute-start(bf16[896,128]{1,0:T(8,128)(2,1)} %refs_0_.3), channel_id=1, source_target_pairs={{0,16},{4,20},{8,24},{12,28},{16,0},{20,4},{24,8},{28,12},{1,17},{... | collective-permute-start | bytes 688136 | tf_op jit(solution)/shard_map/ppermute | solution.py:29
  5.3 16.4 %collective-permute-start.6 = (bf16[896,128]{1,0:T(8,128)(2,1)}, bf16[896,128]{1,0:T(8,128)(2,1)S(1)}, u32[]{:S(2)}, u32[]{:S(2)}) collective-permute-start(bf16[896,128]{1,0:T(8,128)(2,1)} %refs_0_.3), channel_id=1, source_target_pairs={{0,24},{4,28},{8,16},{12,20},{16,8},{20,12},{24,0},{28,4},{1,25},{... | collective-permute-start | bytes 688136 | tf_op jit(solution)/shard_map/ppermute | solution.py:29
  5.3 19.4 %collective-permute-start.3 = (bf16[896,128]{1,0:T(8,128)(2,1)}, bf16[896,128]{1,0:T(8,128)(2,1)S(1)}, u32[]{:S(2)}, u32[]{:S(2)}) collective-permute-start(bf16[896,128]{1,0:T(8,128)(2,1)} %refs_0_.2), channel_id=1, source_target_pairs={{0,8},{4,12},{8,0},{12,4},{16,24},{20,28},{24,16},{28,20},{1,9},{5... | collective-permute-start | bytes 688136 | tf_op jit(solution)/shard_map/ppermute | solution.py:29
  10.4 17.3 %collective-permute-start.1 = (bf16[896,128]{1,0:T(8,128)(2,1)}, bf16[896,128]{1,0:T(8,128)(2,1)S(1)}, u32[]{:S(2)}, u32[]{:S(2)}) collective-permute-start(bf16[896,128]{1,0:T(8,128)(2,1)} %refs_0_.2), channel_id=1, source_target_pairs={{0,16},{4,20},{8,24},{12,28},{16,0},{20,4},{24,8},{28,12},{1,17},{... | collective-permute-start | bytes 688136 | tf_op jit(solution)/shard_map/ppermute | solution.py:29
  12.5 15.2 %collective-permute-start.2 = (bf16[896,128]{1,0:T(8,128)(2,1)}, bf16[896,128]{1,0:T(8,128)(2,1)S(1)}, u32[]{:S(2)}, u32[]{:S(2)}) collective-permute-start(bf16[896,128]{1,0:T(8,128)(2,1)} %refs_0_.2), channel_id=1, source_target_pairs={{0,24},{4,28},{8,16},{12,20},{16,8},{20,12},{24,0},{28,4},{1,25},{... | collective-permute-start | bytes 688136 | tf_op jit(solution)/shard_map/ppermute | solution.py:29
  14.0 4.8 %copy-start = (bf16[896,128]{1,0:T(8,128)(2,1)S(1)}, bf16[896,128]{1,0:T(8,128)(2,1)}, u32[]{:S(2)}) copy-start(bf16[896,128]{1,0:T(8,128)(2,1)} %refs_0_.3) | copy-start | bytes 688132
  21.7 3.1 %copy-start.1 = (bf16[896,128]{1,0:T(8,128)(2,1)S(1)}, bf16[896,128]{1,0:T(8,128)(2,1)}, u32[]{:S(2)}) copy-start(bf16[896,128]{1,0:T(8,128)(2,1)} %refs_0_.2) | copy-start | bytes 688132
  24.6 6.7 %collective-permute-start.8 = (f32[2,288,128]{2,1,0:T(8,128)S(1)}, f32[2,288,128]{2,1,0:T(8,128)S(1)}, u32[]{:S(2)}, u32[]{:S(2)}) collective-permute-start(f32[2,288,128]{2,1,0:T(8,128)S(1)} %shard_map.89.part_ref), channel_id=1, source_target_pairs={{0,4},{4,0},{8,12},{12,8},{16,20},{20,16},{24,28},{28,24},{1,5},{5... | collective-permute-start | bytes 884744 | tf_op jit(solution)/shard_map/ppermute | solution.py:29
  27.6 3.5 %copy-start.4 = (s32[288]{0:T(512)S(1)}, s32[288]{0:T(512)}, u32[]{:S(2)}) copy-start(s32[288]{0:T(512)} %param.10) | copy-start | bytes 3460
  27.6 3.5 %copy-start.5 = (s32[288]{0:T(512)S(1)}, s32[288]{0:T(512)}, u32[]{:S(2)}) copy-start(s32[288]{0:T(512)} %param.11) | copy-start | bytes 3460
  27.6 3.5 %copy-start.6 = (s32[288]{0:T(512)S(1)}, s32[288]{0:T(512)}, u32[]{:S(2)}) copy-start(s32[288]{0:T(512)} %param.13) | copy-start | bytes 3460
  27.7 3.6 %copy-start.3 = (f32[288]{0:T(512)S(1)}, f32[288]{0:T(512)}, u32[]{:S(2)}) copy-start(f32[288]{0:T(512)} %param.12) | copy-start | bytes 3460
  30.6 10.5 %collective-permute-start.4 = (f32[2,288,128]{2,1,0:T(8,128)S(1)}, f32[2,288,128]{2,1,0:T(8,128)S(1)}, u32[]{:S(2)}, u32[]{:S(2)}) collective-permute-start(f32[2,288,128]{2,1,0:T(8,128)S(1)} %shard_map.87.part_ref), channel_id=1, source_target_pairs={{0,4},{4,0},{8,12},{12,8},{16,20},{20,16},{24,28},{28,24},{1,5},{5... | collective-permute-start | bytes 884744 | tf_op jit(solution)/shard_map/ppermute | solution.py:29
  31.3 6.5 %collective-permute-start.9 = (f32[4,288]{1,0:T(4,128)S(1)}, f32[4,288]{1,0:T(4,128)S(1)}, u32[]{:S(2)}, u32[]{:S(2)}) collective-permute-start(f32[4,288]{1,0:T(4,128)S(1)} %pad_maximum_fusion.scalar_ref), channel_id=1, source_target_pairs={{0,4},{4,0},{8,12},{12,8},{16,20},{20,16},{24,28},{28,24},{1,5},{5... | collective-permute-start | bytes 13832 | tf_op jit(solution)/shard_map/ppermute | solution.py:29
  31.5 3.6 %collective-permute-start.10 = (f32[2,128]{1,0:T(2,128)S(1)}, f32[2,128]{1,0:T(2,128)S(1)}, u32[]{:S(2)}, u32[]{:S(2)}) collective-permute-start(f32[2,128]{1,0:T(2,128)S(1)} %get-tuple-element.14.first_ref), channel_id=1, source_target_pairs={{0,1},{1,0},{2,3},{3,2},{4,5},{5,4},{6,7},{7,6},{8,9},{9,8},{10,11... | collective-permute-start | bytes 3080 | tf_op jit(solution)/shard_map/ppermute | solution.py:34
  35.2 4.5 %collective-permute-start.11 = (f32[4,128]{1,0:T(4,128)S(1)}, f32[4,128]{1,0:T(4,128)S(1)}, u32[]{:S(2)}, u32[]{:S(2)}) collective-permute-start(f32[4,128]{1,0:T(4,128)S(1)} %shard_map.91.refs_0_), channel_id=1, source_target_pairs={{0,2},{1,3},{2,0},{3,1},{4,6},{5,7},{6,4},{7,5},{8,10},{9,11},{10,... | collective-permute-start | bytes 6152 | tf_op jit(solution)/shard_map/ppermute | solution.py:34
  43.2 8.3 %collective-permute-start.13 = (bf16[896,128]{1,0:T(8,128)(2,1)S(1)}, bf16[896,128]{1,0:T(8,128)(2,1)S(1)}, u32[]{:S(2)}, u32[]{:S(2)}) collective-permute-start(bf16[896,128]{1,0:T(8,128)(2,1)S(1)} %get-tuple-element.20), channel_id=1, source_target_pairs={{0,16},{4,20},{8,24},{12,28},{16,0},{20,4},{24,8},{28,12},{1,17},{... | collective-permute-start | bytes 688136 | tf_op jit(solution)/shard_map/ppermute | solution.py:29
  44.7 7.9 %collective-permute-start.14 = (bf16[896,128]{1,0:T(8,128)(2,1)S(1)}, bf16[896,128]{1,0:T(8,128)(2,1)S(1)}, u32[]{:S(2)}, u32[]{:S(2)}) collective-permute-start(bf16[896,128]{1,0:T(8,128)(2,1)S(1)} %get-tuple-element.21), channel_id=1, source_target_pairs={{0,8},{4,12},{8,0},{12,4},{16,24},{20,28},{24,16},{28,20},{1,9},{5... | collective-permute-start | bytes 688136 | tf_op jit(solution)/shard_map/ppermute | solution.py:29
  45.3 9.7 %collective-permute-start.12 = (bf16[896,128]{1,0:T(8,128)(2,1)S(1)}, bf16[896,128]{1,0:T(8,128)(2,1)S(1)}, u32[]{:S(2)}, u32[]{:S(2)}) collective-permute-start(bf16[896,128]{1,0:T(8,128)(2,1)S(1)} %get-tuple-element.19), channel_id=1, source_target_pairs={{0,24},{4,28},{8,16},{12,20},{16,8},{20,12},{24,0},{28,4},{1,25},{... | collective-permute-start | bytes 688136 | tf_op jit(solution)/shard_map/ppermute | solution.py:29
  55.2 5.1 %collective-permute-start.15 = (bf16[224,128]{1,0:T(8,128)(2,1)S(1)}, bf16[224,128]{1,0:T(8,128)(2,1)S(1)}, u32[]{:S(2)}, u32[]{:S(2)}) collective-permute-start(bf16[224,128]{1,0:T(8,128)(2,1)S(1)} %get-tuple-element.24), channel_id=1, source_target_pairs={{0,2},{1,3},{2,0},{3,1},{4,6},{5,7},{6,4},{7,5},{8,10},{9,11},{10,... | collective-permute-start | bytes 172040 | tf_op jit(solution)/shard_map/ppermute | solution.py:34
  57.8 6.1 %collective-permute-start.16 = (bf16[224,128]{1,0:T(8,128)(2,1)S(1)}, bf16[224,128]{1,0:T(8,128)(2,1)S(1)}, u32[]{:S(2)}, u32[]{:S(2)}) collective-permute-start(bf16[224,128]{1,0:T(8,128)(2,1)S(1)} %get-tuple-element.26), channel_id=1, source_target_pairs={{0,3},{1,2},{2,1},{3,0},{4,7},{5,6},{6,5},{7,4},{8,11},{9,10},{10,... | collective-permute-start | bytes 172040 | tf_op jit(solution)/shard_map/ppermute | solution.py:34
  59.2 5.1 %collective-permute-start.17 = (bf16[224,128]{1,0:T(8,128)(2,1)S(1)}, bf16[224,128]{1,0:T(8,128)(2,1)S(1)}, u32[]{:S(2)}, u32[]{:S(2)}) collective-permute-start(bf16[224,128]{1,0:T(8,128)(2,1)S(1)} %get-tuple-element.25), channel_id=1, source_target_pairs={{0,1},{1,0},{2,3},{3,2},{4,5},{5,4},{6,7},{7,6},{8,9},{9,8},{10,11... | collective-permute-start | bytes 172040 | tf_op jit(solution)/shard_map/ppermute | solution.py:34
  64.4 5.8 %collective-permute-start.18 = (bf16[224,128]{1,0:T(8,128)(2,1)S(1)}, bf16[224,128]{1,0:T(8,128)(2,1)S(1)}, u32[]{:S(2)}, u32[]{:S(2)}) collective-permute-start(bf16[224,128]{1,0:T(8,128)(2,1)S(1)} %get-tuple-element.23), channel_id=1, source_target_pairs={{0,2},{1,3},{2,0},{3,1},{4,6},{5,7},{6,4},{7,5},{8,10},{9,11},{10,... | collective-permute-start | bytes 172040 | tf_op jit(solution)/shard_map/ppermute | solution.py:34
  66.6 6.0 %collective-permute-start.19 = (bf16[224,128]{1,0:T(8,128)(2,1)S(1)}, bf16[224,128]{1,0:T(8,128)(2,1)S(1)}, u32[]{:S(2)}, u32[]{:S(2)}) collective-permute-start(bf16[224,128]{1,0:T(8,128)(2,1)S(1)} %get-tuple-element.23), channel_id=1, source_target_pairs={{0,3},{1,2},{2,1},{3,0},{4,7},{5,6},{6,5},{7,4},{8,11},{9,10},{10,... | collective-permute-start | bytes 172040 | tf_op jit(solution)/shard_map/ppermute | solution.py:34
  68.6 4.6 %collective-permute-start.20 = (bf16[224,128]{1,0:T(8,128)(2,1)S(1)}, bf16[224,128]{1,0:T(8,128)(2,1)S(1)}, u32[]{:S(2)}, u32[]{:S(2)}) collective-permute-start(bf16[224,128]{1,0:T(8,128)(2,1)S(1)} %get-tuple-element.23), channel_id=1, source_target_pairs={{0,1},{1,0},{2,3},{3,2},{4,5},{5,4},{6,7},{7,6},{8,9},{9,8},{10,11... | collective-permute-start | bytes 172040 | tf_op jit(solution)/shard_map/ppermute | solution.py:34
  73.2 0.8 %copy-start.2 = (f32[896,128]{1,0:T(8,128)}, f32[896,128]{1,0:T(8,128)S(1)}, u32[]{:S(2)}) copy-start(f32[896,128]{1,0:T(8,128)S(1)} %convert_dynamic-update-slice_fusion) | copy-start | bytes 1376260
